TPU v7x, 768 devices: a whole 4x8x12 slice. The times are simulated.
768 devices in a mesh: seq: 48 (over z, x), chan: 16 (over y, core).
Axes of the slice: x: 4, y: 8, z: 12, core: 2. Of those that a mesh axis runs over, the one named last changes fastest.
Arguments:
- query_in: bfloat16 [6144, 2048], P('seq', 'chan'), may hold values from -6 to 6
- key_in: bfloat16 [6144, 2048], P('seq', 'chan'), may hold values from -6 to 6
- value_in: bfloat16 [6144, 2048], P('seq', 'chan'), may hold values from -6 to 6
- short_taps: float32 [3, 7, 2048], P(None, None, 'chan'), may hold values from -2 to 2
- long_filters: bfloat16 [128, 6144], P('chan'), may hold values from -1.1 to 1.1
- skip_gain: float32 [2048], P('chan'), may hold values from -1 to 1
- cotangent: bfloat16 [6144, 2048], P('seq', 'chan'), may hold values from -6 to 6
Outputs:
- block_out: bfloat16 [6144, 2048], P('seq', 'chan')
- input_grads: bfloat16 [3, 6144, 2048], P(None, 'seq', 'chan')
- tap_grads: float32 [3, 7, 2048], P(None, None, 'chan')
- skip_grad: float32 [2048], P('chan')
- filter_grad: float32 [128, 6144], P('chan')
All inputs are finite; a program needn't handle non-finite values.
Results may differ from a plain program's by a relative error of at most 0.0085.
Values may be sent and summed in bfloat16 or wider, within the bound.
A program may use at most 128 MiB of HBM per device.

v0:
```python
import math

import jax
import jax.numpy as jnp
from jax import lax
from jax.sharding import PartitionSpec as P


def from_behind(value, axis, steps):
    count = lax.axis_size(axis)
    initial, last = (max(0, -steps), min(count, count - steps))
    return lax.ppermute(value, axis, [(source, source + steps) for source in range(initial, last)])


def short_forward(extended, weights, rows_here):
    margin = weights.shape[0] - 1
    running = jnp.zeros((rows_here, extended.shape[1]), jnp.float32)
    for offset in range(weights.shape[0]):
        running = (
            running + weights[offset] * extended[margin - offset : margin - offset + rows_here]
        )
    return running


def short_backward(extended, weights, rows_here):
    running = jnp.zeros((rows_here, extended.shape[1]), jnp.float32)
    for offset in range(weights.shape[0]):
        running = running + weights[offset] * extended[offset : offset + rows_here]
    return running


def tap_sums(grad_rows, extended, tap_count, rows_here):
    margin = tap_count - 1
    sums_list = []
    for offset in range(tap_count):
        sums_list.append(
            jnp.sum(grad_rows * extended[margin - offset : margin - offset + rows_here], axis=0)
        )
    return jnp.stack(sums_list)


def hankel(padded, lag_start, height, breadth, seq_total):
    span = height + breadth - 1
    window = lax.dynamic_slice_in_dim(padded, lag_start + seq_total, span, axis=1)
    tiled = jnp.tile(window, (1, height))
    tiled = jnp.pad(tiled, ((0, 0), (0, height)))
    return tiled.reshape(padded.shape[0], height, span + 1)[:, :, :breadth]


def causal_part(padded, source_rows, source_start, target_start, target_count, seq_total):
    breadth = source_rows.shape[0]
    matrix = hankel(
        padded, target_start - source_start - breadth + 1, target_count, breadth, seq_total
    )
    return jnp.einsum("gts,sgc->tgc", matrix, source_rows[::-1], preferred_element_type=jnp.float32)


def anti_part(padded, target_rows, target_start, source_start, source_count, seq_total):
    breadth = target_rows.shape[0]
    matrix = hankel(
        padded, target_start - source_start - source_count + 1, source_count, breadth, seq_total
    )
    return jnp.einsum("gab,bgc->agc", matrix, target_rows, preferred_element_type=jnp.float32)[::-1]


def lag_part(buffer, target_rows, source_rows, target_start, source_start, seq_total):
    height = target_rows.shape[0]
    breadth = source_rows.shape[0]
    groups = target_rows.shape[1]
    padded_source = jnp.pad(source_rows[::-1], ((0, height), (0, 0), (0, 0)))
    products = jnp.einsum(
        "tgc,sgc->gts", target_rows, padded_source, preferred_element_type=jnp.float32
    )
    full_width = height + breadth
    skewed = products.reshape(groups, height * full_width)[:, : height * (full_width - 1)]
    skewed = skewed.reshape(groups, height, full_width - 1)
    diagonal = jnp.sum(skewed, axis=1)
    position = target_start - source_start - breadth + 1 + seq_total
    current = lax.dynamic_slice_in_dim(buffer, position, full_width - 1, axis=1)
    return lax.dynamic_update_slice_in_dim(buffer, current + diagonal, position, axis=1)


def local(query_in, key_in, value_in, short_taps, long_filters, skip_gain, cotangent):
    tok_rows, chan_width = query_in.shape
    groups, seq_total = long_filters.shape
    members = chan_width // groups
    tap_count = short_taps.shape[1]
    margin = tap_count - 1
    device = lax.axis_index("seq")
    own_start = device * tok_rows
    rim_rows = jnp.stack(
        [query_in[tok_rows - margin :], key_in[tok_rows - margin :], value_in[tok_rows - margin :]]
    )
    before = from_behind(rim_rows, "seq", 1)
    streams = [query_in, key_in, value_in]
    extended = [
        jnp.concatenate([before[stream], streams[stream]]).astype(jnp.float32)
        for stream in range(3)
    ]
    query_short = short_forward(extended[0], short_taps[0], tok_rows)
    key_short = short_forward(extended[1], short_taps[1], tok_rows)
    value_short = short_forward(extended[2], short_taps[2], tok_rows)
    gating = (key_short * value_short).astype(jnp.bfloat16)
    relayed = (cotangent.astype(jnp.float32) * query_short).astype(jnp.bfloat16)
    gating_wide = gating.astype(jnp.float32)
    relayed_wide = relayed.astype(jnp.float32)
    gating_groups = gating.reshape(tok_rows, groups, members)
    relayed_groups = relayed.reshape(tok_rows, groups, members)
    padded = jnp.concatenate([jnp.zeros((groups, seq_total), jnp.bfloat16), long_filters], axis=1)
    lag_buffer = jnp.zeros((groups, 2 * seq_total), jnp.float32)
    zeros_out = jnp.zeros((tok_rows, groups, members), jnp.float32)

    def target_pair(distance):
        return distance < 0

    totals = (zeros_out, lag_buffer)
    shard_rows = lax.all_gather(gating, "seq", axis=0, tiled=True)
    piece_rows = shard_rows.shape[0]
    step_rows = min(piece_rows, tok_rows)
    pieces = shard_rows.reshape(piece_rows // step_rows, step_rows, groups, members)

    def forward_visit_block(carried, element):
        position, rows_block = element
        source_start = position * step_rows

        def forward_active(partial_value):
            output_part, buffer = partial_value
            output_part = output_part + causal_part(
                padded, rows_block, source_start, own_start, tok_rows, seq_total
            )
            distance = device - source_start // tok_rows
            buffer = lax.cond(
                target_pair(distance),
                lambda held: lag_part(
                    held, relayed_groups, rows_block, own_start, source_start, seq_total
                ),
                lambda held: held,
                buffer,
            )
            return (output_part, buffer)

        carried = lax.cond(
            source_start < own_start + tok_rows,
            forward_active,
            lambda partial_value: partial_value,
            carried,
        )
        return (carried, None)

    totals, ignored = lax.scan(
        forward_visit_block, totals, (jnp.arange(piece_rows // step_rows, dtype=jnp.int32), pieces)
    )
    output_part, lag_buffer = totals
    output_sum = output_part.reshape(tok_rows, chan_width)
    totals = (zeros_out, lag_buffer)
    shard_rows = lax.all_gather(relayed, "seq", axis=0, tiled=True)
    piece_rows = shard_rows.shape[0]
    backward_step_rows = min(piece_rows, tok_rows)
    pieces = shard_rows.reshape(
        piece_rows // backward_step_rows, backward_step_rows, groups, members
    )

    def backward_visit_block(carried, element):
        position, rows_block = element
        target_start = position * backward_step_rows

        def backward_active(partial_value):
            grad_part, buffer = partial_value
            grad_part = grad_part + anti_part(
                padded, rows_block, target_start, own_start, tok_rows, seq_total
            )
            distance = target_start // tok_rows - device
            buffer = lax.cond(
                target_pair(distance),
                lambda held: held,
                lambda held: lag_part(
                    held, rows_block, gating_groups, target_start, own_start, seq_total
                ),
                buffer,
            )
            return (grad_part, buffer)

        carried = lax.cond(
            target_start + backward_step_rows > own_start,
            backward_active,
            lambda partial_value: partial_value,
            carried,
        )
        return (carried, None)

    totals, ignored = lax.scan(
        backward_visit_block,
        totals,
        (jnp.arange(piece_rows // backward_step_rows, dtype=jnp.int32), pieces),
    )
    grad_part, lag_buffer = totals
    grad_sum = grad_part.reshape(tok_rows, chan_width)
    lag_local = lag_buffer[:, seq_total:]
    long_out = output_sum + skip_gain * gating_wide
    block_out = (query_short * long_out).astype(jnp.bfloat16)
    grad_gating = grad_sum + skip_gain * relayed_wide
    cot_wide = cotangent.astype(jnp.float32)
    grad_shorts = [cot_wide * long_out, grad_gating * value_short, grad_gating * key_short]
    lead_rows = jnp.stack([grad_shorts[stream][:margin] for stream in range(3)])
    after = from_behind(lead_rows, "seq", -1)
    input_grads = jnp.stack(
        [
            short_backward(
                jnp.concatenate([grad_shorts[stream], after[stream]]), short_taps[stream], tok_rows
            )
            for stream in range(3)
        ]
    ).astype(jnp.bfloat16)
    tap_local = jnp.stack(
        [
            tap_sums(grad_shorts[stream], extended[stream], tap_count, tok_rows)
            for stream in range(3)
        ]
    )
    skip_local = jnp.sum(relayed_wide * gating_wide, axis=0)
    lag_total, tap_total, skip_total = lax.psum((lag_local, tap_local, skip_local), "seq")
    tap_scale = 1.0 / math.sqrt(seq_total)
    lag_scale = 1.0 / math.sqrt(seq_total * members)
    return (
        block_out,
        input_grads,
        tap_total * tap_scale,
        skip_total * tap_scale,
        lag_total * lag_scale,
    )


def solution(mesh):
    in_specs = (
        P("seq", "chan"),
        P("seq", "chan"),
        P("seq", "chan"),
        P(None, None, "chan"),
        P("chan", None),
        P("chan"),
        P("seq", "chan"),
    )
    out_specs = (
        P("seq", "chan"),
        P(None, "seq", "chan"),
        P(None, None, "chan"),
        P("chan"),
        P("chan", None),
    )
    return jax.shard_map(local, mesh=mesh, in_specs=in_specs, out_specs=out_specs, check_vma=False)
```

profile of v0, /device:TPU:56, one launch (start us, length us, event | category | flops | bytes accessed | tf_op | source)
XLA Modules:
  0.0 1034.9 jit_solution(12472849380217231466)
XLA Ops:
  20.9 116.2 %all-gather.3.cloned.1.call-done = bf16[6144,128]{0,1:T(8,128)(2,1)} async-done(((bf16[128,128]{0,1:T(8,128)(2,1)}), bf16[6144,128]{0,1:T(8,128)(2,1)}) %all-gather.3.cloned.1.call-update) | async-done | bytes 1572880 | tf_op jit(solution)/shard_map/all_gather | solution.py:117
  140.6 66.3 %while.31 = (s32[]{:T(128)}, f32[128,8,16]{0,2,1:T(8,128)S(1)}, f32[8,12288]{1,0:T(8,128)S(1)}, s32[48]{0:T(128)S(1)}, s32[]{:T(128)}, /*index=5*/s32[]{:T(128)}...) while((s32[]{:T(128)}, f32[128,8,16]{0,2,1:T(8,128)S(1)}, ...), condition=%wide.region_6.7_spmd, body=%wide.region_0.6_spmd.sunk | while | flops 12860449 | bytes 14877061 | solution.py:150
  206.9 43.3 %all-gather.5.cloned.1.call-done = bf16[6144,128]{0,1:T(8,128)(2,1)} async-done(((bf16[128,128]{0,1:T(8,128)(2,1)}), bf16[6144,128]{0,1:T(8,128)(2,1)}) %all-gather.5.cloned.1.call-update) | async-done | bytes 1572880 | tf_op jit(solution)/shard_map/all_gather | solution.py:156
  254.0 354.6 %while.32 = (s32[]{:T(128)}, f32[128,8,16]{0,2,1:T(8,128)S(1)}, f32[8,12288]{1,0:T(8,128)S(1)}, s32[48]{0:T(128)}, s32[]{:T(128)}, /*index=5*/bf16[8,12288]{1,0:...) while((s32[]{:T(128)}, f32[128,8,16]{0,2,1:T(8,128)S(1)}, ...), condition=%wide.region_13.14_spmd, body=%wide.region_7.13_spmd.sunk | while | flops 12860450 | bytes 15073681 | solution.py:191
  270.7 5.5 conditional.7
  278.1 5.5 conditional.7
  285.5 5.5 conditional.7
  292.9 5.5 conditional.7
  315.0 5.5 conditional.7
  322.4 5.5 conditional.7
  337.2 5.5 conditional.7
  359.4 5.5 conditional.7
  381.5 5.5 conditional.7
  403.7 5.5 conditional.7
  425.9 5.5 conditional.7
  448.0 5.5 conditional.7
  470.2 5.5 conditional.7
  492.4 5.5 conditional.7
  514.5 5.5 conditional.7
  536.7 5.5 conditional.7
  558.9 5.5 conditional.7
  581.0 5.5 conditional.7
  611.1 205.8 %all-reduce.5 = (f32[3,7,128]{2,1,0:T(8,128)S(1)}, f32[128]{0:T(128)S(1)}) all-reduce(f32[3,7,128]{2,1,0:T(8,128)S(1)} %pad_maximum_fusion.5, f32[128]{0:T(128)S(1)} %copy-done.37), channel_id=1, replica_groups=mesh['seq'=48,'chan'=16] {'seq'}, use_global_device_ids=true, to_apply=%region_35.36 | all-reduce | flops 2816 | bytes 22528 | tf_op jit(solution)/shard_map/psum | solution.py:221
  827.3 199.4 %all-reduce.8.cloned.1.call-done = f32[8,6144]{1,0:T(8,128)} async-done(((f32[8,6144]{1,0:T(8,128)}), f32[8,6144]{1,0:T(8,128)}) %all-reduce.8.cloned.1.call-update) | async-done | bytes 196624 | tf_op jit(solution)/shard_map/psum | solution.py:221
  (1227 shorter events, 710.0 us)
Async XLA Ops:
  7.2 13.7 %copy-start.2 = (bf16[8,6144]{1,0:T(8,128)(2,1)S(1)}, bf16[8,6144]{1,0:T(8,128)(2,1)}, u32[]{:S(2)}) copy-start(bf16[8,6144]{1,0:T(8,128)(2,1)} %param.23) | copy-start | bytes 294916
  7.2 130.0 %all-gather.3.cloned.1.call-start = ((), (), s32[]{:S(2)}) async-start(), calls=%async_computation | async-start | bytes 1605632 | tf_op jit(solution)/shard_map/all_gather | solution.py:117
  8.8 8.8 collective-permute-start
  13.3 7.6 copy-start.3
  19.9 230.3 %all-gather.5.cloned.1.call-start = ((), (), s32[]{:S(2)}) async-start(), calls=%async_computation.1 | async-start | bytes 1605632 | tf_op jit(solution)/shard_map/all_gather | solution.py:156
  20.7 1006.1 %all-reduce.8.cloned.1.call-start = ((), (), s32[]{:S(2)}) async-start(), calls=%async_computation.2 | async-start | bytes 393216 | tf_op jit(solution)/shard_map/psum | solution.py:221
  609.6 215.6 %copy-start.20 = (f32[128]{0:T(128)S(1)}, f32[128]{0:T(128)}, u32[]{:S(2)}) copy-start(f32[128]{0:T(128)} %copy-done.19) | copy-start | bytes 1540
  609.6 215.6 %copy-start.22 = (f32[128]{0:T(128)S(1)}, f32[128]{0:T(128)}, u32[]{:S(2)}) copy-start(f32[128]{0:T(128)} %copy-done.21) | copy-start | bytes 1540
  609.6 215.6 %copy-start.24 = (f32[128]{0:T(128)S(1)}, f32[128]{0:T(128)}, u32[]{:S(2)}) copy-start(f32[128]{0:T(128)} %copy-done.23) | copy-start | bytes 1540
  609.7 215.6 %copy-start.26 = (f32[128]{0:T(128)S(1)}, f32[128]{0:T(128)}, u32[]{:S(2)}) copy-start(f32[128]{0:T(128)} %copy-done.25) | copy-start | bytes 1540
  609.7 215.6 %copy-start.28 = (f32[128]{0:T(128)S(1)}, f32[128]{0:T(128)}, u32[]{:S(2)}) copy-start(f32[128]{0:T(128)} %copy-done.27) | copy-start | bytes 1540
  609.7 215.6 %copy-start.30 = (f32[128]{0:T(128)S(1)}, f32[128]{0:T(128)}, u32[]{:S(2)}) copy-start(f32[128]{0:T(128)} %copy-done.29) | copy-start | bytes 1540
  609.7 215.6 %copy-start.32 = (f32[128]{0:T(128)S(1)}, f32[128]{0:T(128)}, u32[]{:S(2)}) copy-start(f32[128]{0:T(128)} %copy-done.31) | copy-start | bytes 1540
  609.7 216.0 %copy-start.6 = (f32[128]{0:T(128)S(1)}, f32[128]{0:T(128)}, u32[]{:S(2)}) copy-start(f32[128]{0:T(128)} %copy-done.5) | copy-start | bytes 1540
  609.7 216.0 %copy-start.8 = (f32[128]{0:T(128)S(1)}, f32[128]{0:T(128)}, u32[]{:S(2)}) copy-start(f32[128]{0:T(128)} %copy-done.7) | copy-start | bytes 1540
  609.7 216.0 %copy-start.10 = (f32[128]{0:T(128)S(1)}, f32[128]{0:T(128)}, u32[]{:S(2)}) copy-start(f32[128]{0:T(128)} %copy-done.9) | copy-start | bytes 1540
  609.7 216.0 %copy-start.12 = (f32[128]{0:T(128)S(1)}, f32[128]{0:T(128)}, u32[]{:S(2)}) copy-start(f32[128]{0:T(128)} %copy-done.11) | copy-start | bytes 1540
  609.7 216.0 %copy-start.14 = (f32[128]{0:T(128)S(1)}, f32[128]{0:T(128)}, u32[]{:S(2)}) copy-start(f32[128]{0:T(128)} %copy-done.13) | copy-start | bytes 1540
  609.8 216.0 %copy-start.16 = (f32[128]{0:T(128)S(1)}, f32[128]{0:T(128)}, u32[]{:S(2)}) copy-start(f32[128]{0:T(128)} %copy-done.15) | copy-start | bytes 1540
  609.8 216.0 %copy-start.18 = (f32[128]{0:T(128)S(1)}, f32[128]{0:T(128)}, u32[]{:S(2)}) copy-start(f32[128]{0:T(128)} %copy-done.17) | copy-start | bytes 1540
  609.8 216.4 %copy-start.4 = (f32[128]{0:T(128)S(1)}, f32[128]{0:T(128)}, u32[]{:S(2)}) copy-start(f32[128]{0:T(128)} %copy-done.3) | copy-start | bytes 1540
  609.8 216.4 %copy-start.34 = (f32[128]{0:T(128)S(1)}, f32[128]{0:T(128)}, u32[]{:S(2)}) copy-start(f32[128]{0:T(128)} %copy-done.33) | copy-start | bytes 1540
  609.8 216.4 %copy-start.36 = (f32[128]{0:T(128)S(1)}, f32[128]{0:T(128)}, u32[]{:S(2)}) copy-start(f32[128]{0:T(128)} %copy-done.35) | copy-start | bytes 1540
  817.6 7.6 collective-permute-start.1
  (19 other events, 125.7 us)
Sparse Core Ops, SparseCore 0:
  20.0 117.0 all-gather.2
  141.3 108.8 all-gather.4
  820.3 206.4 all-reduce.7
where the time goes:
time: 1040 us; the launch traced here: 1030 us
  waiting for transfers between devices  364 us (35%)
  local copies, waits for them, and re-layouts  328 us (32%)
  blocking collectives  206 us (20%)
  loops' own time  72.3 us (7%)
  matrix products  28.1 us (3%)
  other arithmetic  17.6 us (2%)
  between operations  14.5 us (1%)
    psum x1, blocking collectives, local(): lax.psum((lag_local, tap_local, skip_local), 'seq')  206 us
    psum x1, waiting for transfers between devices, local(): lax.psum((lag_local, tap_local, skip_local), 'seq')  199 us
    all_gather x1, waiting for transfers between devices, local(): shard_rows = lax.all_gather(gating, 'seq', axis=0, tiled=True)  116 us
    dynamic_slice x96, local copies, waits for them, and re-layouts, local(): lax.scan(forward_visit_block, totals, (jnp.arange(piece_rows // step_rows...  91 us
    reshape x48, local copies, waits for them, and re-layouts, lag_part(): skewed = skewed.reshape(groups, height, full_width - 1)  67.3 us
    all_gather x1, waiting for transfers between devices, local(): shard_rows = lax.all_gather(relayed, 'seq', axis=0, tiled=True)  43.3 us
    squeeze x49, local copies, waits for them, and re-layouts, local(): lax.scan(forward_visit_block, totals, (jnp.arange(piece_rows // step_rows...  37.6 us
    cond x97, local copies, waits for them, and re-layouts  34.4 us
  transfers between devices with their start and end apart: 5, of which 4 were waited for; matrix products, arithmetic and copies ran while one was open for 4% of the time, Pallas kernels for 0%

commit v1 on v0

v1 whole, which is shorter than its diff:
```python
import math

import jax
import jax.numpy as jnp
from jax import lax
from jax.experimental import pallas as pl
from jax.experimental.pallas import tpu as pltpu
from jax.sharding import PartitionSpec as P

F32 = jnp.float32
BF16 = jnp.bfloat16
MESH = pl.DeviceIdType.MESH

BLK = 128
NB = 48
NW = 32
TAPS = 7
NG = 8
QUART = NB // 4
PAIRS = NB // 2


def worker_of(index):
    z, x = index // 4, index % 4
    return ((z // 3) * 2 + z % 3) * 4 + x


def is_worker(index):
    return (index // 4) % 3 != 2


def index_of(worker):
    group, x = worker // 4, worker % 4
    return ((group // 2) * 3 + group % 2) * 4 + x


def iota(shape, dim):
    return lax.broadcasted_iota(jnp.int32, shape, dim)


def dot(a, b, dims=((1,), (0,))):
    return lax.dot_general(a, b, (dims, ((), ())), preferred_element_type=F32)


def half_turn(x):
    return pltpu.roll(x, 4, 0)


def remote(src, dst, send_sem, recv_sem, target):
    return pltpu.make_async_remote_copy(
        src_ref=src,
        dst_ref=dst,
        send_sem=send_sem,
        recv_sem=recv_sem,
        device_id={"seq": target},
        device_id_type=MESH,
    )


def kernel(
    q_ref, k_ref, v_ref, c_ref, taps_ref, filt_ref, skip_ref,
    out_ref, ig_ref, tapg_ref, skipg_ref, fg_ref,
    perm, sendb, recvb, toep, tcol, conv_s, pb_s, pbj_s, r8_s, gg_s, z_s, y_s, yj_s,
    retb, retr, small, smallr, sm_s, fbuf, frecv, fq, fgbuf,
    in_send, in_recv, ret_send, ret_recv, sm_send, sm_recv,
    fr_send, fr_recv, fb_send, fb_recv,
):
    me = lax.axis_index("seq")
    mine = worker_of(me)
    group = mine // 4
    part = me % 4
    tap_scale = 1.0 / math.sqrt(NB * BLK)
    lag_scale = 1.0 / math.sqrt(NB * BLK * 16)

    barrier = pltpu.get_barrier_semaphore()

    def greet(i, carry):
        pl.semaphore_signal(
            barrier, inc=1, device_id={"seq": lax.rem(me + i, NB)}, device_id_type=MESH
        )
        return carry

    lax.fori_loop(1, NB, greet, 0)

    rho = iota((512, 1), 0)
    target_col = 128 * ((rho // 4) % 4) + 4 * (rho // 16) + rho % 4
    perm[...] = jnp.where(iota((512, 512), 1) == target_col, 1.0, 0.0).astype(BF16)
    streams = jnp.concatenate([q_ref[...], k_ref[...], c_ref[...], v_ref[...]], axis=1)
    sendb[...] = dot(perm[...], streams, ((1,), (1,))).astype(BF16).reshape(NW, 16, BLK)

    pl.semaphore_wait(barrier, NB - 1)

    def send_in(i, carry):
        target = lax.rem(me + i, NB)

        @pl.when(is_worker(target))
        def _():
            worker = worker_of(target)
            remote(
                sendb.at[worker], recvb.at[me], in_send.at[worker], in_recv.at[me], target
            ).start()

        return carry

    lax.fori_loop(1, NB, send_in, 0)

    @pl.when(is_worker(me))
    def _work():
        lane = iota((16, BLK), 1)
        row = iota((16, BLK), 0)
        low_rows = iota((8, BLK), 0) < 4

        own = lane == 4 * mine + row % 4
        for j in range(TAPS):
            q_tap = jnp.broadcast_to(taps_ref[0, j : j + 1, :], (16, BLK))
            k_tap = jnp.broadcast_to(taps_ref[1, j : j + 1, :], (16, BLK))
            v_tap = jnp.broadcast_to(taps_ref[2, j : j + 1, :], (16, BLK))
            tap = jnp.where(row < 4, q_tap, jnp.where(row < 8, k_tap, v_tap))
            column = jnp.sum(jnp.where(own, tap, 0.0), axis=1, keepdims=True)
            column = jnp.broadcast_to(column, (16, BLK))
            unit = 1.0 if j == 0 else 0.0
            tcol[j] = jnp.where((row >= 8) & (row < 12), unit, column)
        skip_own = jnp.where(own, jnp.broadcast_to(skip_ref[...], (16, BLK)), 0.0)
        skip_col = jnp.broadcast_to(jnp.sum(skip_own, axis=1, keepdims=True), (16, BLK))[:8]

        square_row = iota((BLK, BLK), 0)
        square_lane = iota((BLK, BLK), 1)
        toep[0] = jnp.zeros((BLK, BLK), BF16)

        def build(n, previous):
            rows = filt_ref[:, pl.ds(pl.multiple_of(n * BLK, BLK), BLK)].astype(F32)
            line = jnp.sum(jnp.where(iota((NG, BLK), 0) == group, rows, 0.0), axis=0, keepdims=True)
            turned = pltpu.roll(
                jnp.broadcast_to(line, (BLK, BLK)), 0, 1, stride=1, stride_axis=0
            )
            toep[n + 1] = jnp.where(square_lane >= square_row, turned, previous).astype(BF16)
            return turned

        lax.fori_loop(0, NB, build, jnp.zeros((BLK, BLK), F32))
        flip = jnp.where(square_row + square_lane == BLK - 1, 1.0, 0.0).astype(BF16)

        r8_s[PAIRS:] = jnp.zeros((32 - PAIRS, 8, BLK), F32)
        gg_s[:PAIRS] = jnp.zeros((PAIRS, 8, 2 * BLK), F32)
        gg_s[2 * PAIRS :] = jnp.zeros((32 - PAIRS, 8, 2 * BLK), F32)
        y_s[...] = jnp.zeros((2 * PAIRS, 8, 2 * BLK), F32)
        pbj_s[0] = jnp.zeros((8, BLK), F32)

        recvb[me] = sendb[mine]

        def short(b, before):
            @pl.when(b != me)
            def _():
                remote(
                    sendb.at[0], recvb.at[b], in_send.at[0], in_recv.at[b], b
                ).wait_recv()

            x = recvb[b].astype(F32)
            total = tcol[0] * x
            turned = []
            for j in range(1, TAPS):
                t = pltpu.roll(x, j, 1)
                total = total + tcol[j] * jnp.where(lane < j, before[j - 1], t)
                turned.append(t)
            conv_s[b] = total
            pb_s[b] = (total[:8] * total[8:]).astype(BF16).astype(F32)
            return tuple(turned)

        empty = tuple(jnp.zeros((16, BLK), F32) for _ in range(TAPS - 1))
        lax.fori_loop(0, NB, short, empty)

        pbj_s[1:] = dot(pb_s[...].reshape(NB * 8, BLK).astype(BF16), flip).reshape(NB, 8, BLK)

        def arrange(e, carry):
            p0, p1 = pb_s[2 * e], pb_s[2 * e + 1]
            jm, j0, j1 = pbj_s[2 * e], pbj_s[2 * e + 1], pbj_s[2 * e + 2]
            r8_s[e] = jnp.where(low_rows, p0, half_turn(p1))
            gg_s[PAIRS + e, :, :BLK] = jnp.where(low_rows, half_turn(j0), j1)
            gg_s[PAIRS + e, :, BLK:] = jnp.where(low_rows, half_turn(jm), j0)
            z_s[e, :, :BLK] = jnp.where(low_rows, pbj_s[NB - 2 * e], p0)
            z_s[e, :, BLK:] = jnp.where(low_rows, pbj_s[NB - 1 - 2 * e], p1)
            return carry

        lax.fori_loop(0, PAIRS, arrange, 0)

        unit = jnp.where(square_row == square_lane, 1.0, 0.0).astype(BF16)
        r8_t = dot(unit, r8_s[...].reshape(256, BLK).astype(BF16), ((1,), (1,))).astype(BF16)
        inside = square_lane <= square_row

        def lags(f, previous):
            shifted = gg_s[pl.ds(PAIRS - f, 32)].reshape(256, 2 * BLK).astype(BF16)
            product = dot(r8_t, shifted)
            even = pltpu.roll(product[:, :BLK], 1, 1, stride=1, stride_axis=0)
            odd = pltpu.roll(product[:, BLK:], 1, 1, stride=1, stride_axis=0)
            fbuf[2 * f] = jnp.sum(jnp.where(inside, previous, even), axis=0, keepdims=True)
            fbuf[2 * f + 1] = jnp.sum(jnp.where(inside, even, odd), axis=0, keepdims=True)
            return odd

        last = lax.fori_loop(0, PAIRS, lags, jnp.zeros((BLK, BLK), F32))
        fbuf[NB] = jnp.sum(jnp.where(inside, last, 0.0), axis=0, keepdims=True)

        def send_lags(i, carry):
            other = lax.rem(part + i, 4)
            remote(
                fbuf.at[pl.ds(1 + QUART * other, QUART)], frecv.at[part],
                fr_send.at[other], fr_recv.at[part], me - part + other,
            ).start()
            return carry

        lax.fori_loop(1, 4, send_lags, 0)

        z = z_s[...].reshape(PAIRS * 8, 2 * BLK).astype(BF16)

        def convolve(d, carry):
            t0, t1, t2 = toep[2 * d], toep[2 * d + 1], toep[2 * d + 2]
            weights = jnp.concatenate(
                [jnp.concatenate([t1, t2], axis=1), jnp.concatenate([t0, t1], axis=1)], axis=0
            )
            y_s[pl.ds(d, PAIRS)] += dot(z, weights).reshape(PAIRS, 8, 2 * BLK)
            return carry

        lax.fori_loop(0, PAIRS, convolve, 0)

        for half in range(2):
            y = y_s[:PAIRS, :, half * BLK : (half + 1) * BLK].reshape(PAIRS * 8, BLK)
            high = y.astype(BF16)
            rest = (y - high.astype(F32)).astype(BF16)
            yj_s[:, :, half * BLK : (half + 1) * BLK] = (
                dot(high, flip) + dot(rest, flip)
            ).reshape(PAIRS, 8, BLK)

        def finish(b, y, yj, after, sums, skip_sum):
            p = pb_s[b]
            u = half_turn(jnp.where(low_rows, yj, y) + skip_col * p)
            short_tile = conv_s[b]
            he = jnp.concatenate([short_tile[8:] * u, short_tile[:8] * u], axis=0)
            x = recvb[b].astype(F32)
            total = tcol[0] * he
            new_sums = [sums[0] + he * x]
            turned = []
            for j in range(1, TAPS):
                t = pltpu.roll(he, BLK - j, 1)
                s = jnp.where(lane < BLK - j, t, after[j - 1])
                total = total + tcol[j] * s
                new_sums.append(sums[j] + s * x)
                turned.append(t)
            retb[b] = total.astype(BF16)
            return tuple(turned), tuple(new_sums), skip_sum + p * half_turn(p)

        def send_back(b):
            @pl.when(b != me)
            def _():
                remote(retb.at[b], retr.at[mine], ret_send.at[b], ret_recv.at[mine], b).start()

        def post(i, carry):
            after, sums, skip_sum = carry
            e = PAIRS - 1 - i
            after, sums, skip_sum = finish(
                2 * e + 1, y_s[e, :, BLK:], yj_s[i, :, :BLK], after, sums, skip_sum
            )
            after, sums, skip_sum = finish(
                2 * e, y_s[e, :, :BLK], yj_s[i, :, BLK:], after, sums, skip_sum
            )
            return after, sums, skip_sum

        start = (
            empty,
            tuple(jnp.zeros((16, BLK), F32) for _ in range(TAPS)),
            jnp.zeros((8, BLK), F32),
        )
        _, sums, skip_sum = lax.fori_loop(0, PAIRS, post, start)

        def return_block(i, carry):
            send_back(lax.rem(me + i, NB))
            return carry

        lax.fori_loop(1, NB, return_block, 0)

        line = jnp.zeros((16, BLK), F32)
        for j in range(TAPS):
            line = line + jnp.where(
                lane == 16 * j + row, jnp.sum(sums[j], axis=1, keepdims=True), 0.0
            )
        skip_line = jnp.where(
            lane[:8] == 16 * TAPS + row[:8], jnp.sum(skip_sum, axis=1, keepdims=True), 0.0
        )
        small[...] = tap_scale * (
            jnp.sum(line, axis=0, keepdims=True) + jnp.sum(skip_line, axis=0, keepdims=True)
        )

        frecv[part] = fbuf[pl.ds(1 + QUART * part, QUART)]

        def wait_lags(i, carry):
            other = lax.rem(part + i, 4)
            remote(
                fbuf.at[pl.ds(0, QUART)], frecv.at[other],
                fr_send.at[0], fr_recv.at[other], me - part + other,
            ).wait_recv()
            return carry

        lax.fori_loop(1, 4, wait_lags, 0)
        fq[...] = lag_scale * ((frecv[0] + frecv[1]) + (frecv[2] + frecv[3]))

        def broadcast(i, carry):
            target = lax.rem(me + i, NB)
            remote(small, smallr.at[mine], sm_send.at[target], sm_recv.at[mine], target).start()
            remote(
                fq, fgbuf.at[group, pl.ds(QUART * part, QUART)],
                fb_send.at[target], fb_recv.at[mine], target,
            ).start()
            return carry

        lax.fori_loop(1, NB, broadcast, 0)
        retr[mine] = retb[me]
        smallr[mine] = small[...]
        fgbuf[group, pl.ds(QUART * part, QUART)] = fq[...]

    def wait_back(m, carry):
        source = index_of(m)

        @pl.when(source != me)
        def _():
            remote(retb.at[0], retr.at[m], ret_send.at[0], ret_recv.at[m], source).wait_recv()

        return carry

    lax.fori_loop(0, NW, wait_back, 0)
    back = dot(retr[...].reshape(512, BLK), perm[...], ((0,), (0,))).astype(BF16)
    ig_ref[0] = back[:, 0:128]
    ig_ref[1] = back[:, 128:256]
    out_ref[...] = back[:, 256:384]
    ig_ref[2] = back[:, 384:512]

    def wait_small(m, carry):
        source = index_of(m)

        @pl.when(source != me)
        def _():
            remote(small, smallr.at[m], sm_send.at[0], sm_recv.at[m], source).wait_recv()
            remote(
                fq, fgbuf.at[m // 4, pl.ds(QUART * (m % 4), QUART)],
                fb_send.at[0], fb_recv.at[m], source,
            ).wait_recv()

        return carry

    lax.fori_loop(0, NW, wait_small, 0)

    sm_s[...] = jnp.zeros((BLK, BLK), F32)
    for m in range(NW):
        sm_s[m : m + 1, :] = smallr[m]
    select = jnp.where(iota((BLK, BLK), 0) == iota((BLK, BLK), 1) // 4, 1.0, 0.0)
    spread = lax.dot_general(
        sm_s[...].T, select, (((1,), (0,)), ((), ())),
        precision=lax.Precision.HIGHEST, preferred_element_type=F32,
    ).reshape(8, 16, BLK)
    row3 = iota((8, 16, BLK), 1)
    channel = iota((8, 16, BLK), 2) % 4
    for stream, first in enumerate((0, 4, 12)):
        picked = jnp.sum(jnp.where(row3 == channel + first, spread, 0.0), axis=1)
        tapg_ref[stream] = picked[:TAPS]
        if stream == 0:
            skipg_ref[...] = picked[TAPS:]

    def lay(n, carry):
        for g in range(NG):
            fg_ref[g : g + 1, pl.ds(pl.multiple_of(n * BLK, BLK), BLK)] = fgbuf[g, n]
        return carry

    lax.fori_loop(0, NB, lay, 0)

    def drain_in(i, carry):
        target = lax.rem(me + i, NB)

        @pl.when(is_worker(target))
        def _():
            worker = worker_of(target)
            remote(
                sendb.at[worker], recvb.at[me], in_send.at[worker], in_recv.at[me], target
            ).wait_send()

        return carry

    lax.fori_loop(1, NB, drain_in, 0)

    @pl.when(is_worker(me))
    def _drain():
        def drain_lags(i, carry):
            other = lax.rem(part + i, 4)
            remote(
                fbuf.at[pl.ds(1 + QUART * other, QUART)], frecv.at[part],
                fr_send.at[other], fr_recv.at[part], me - part + other,
            ).wait_send()
            return carry

        lax.fori_loop(1, 4, drain_lags, 0)

        def drain(i, carry):
            target = lax.rem(me + i, NB)
            remote(
                retb.at[target], retr.at[mine], ret_send.at[target], ret_recv.at[mine], target
            ).wait_send()
            remote(
                small, smallr.at[mine], sm_send.at[target], sm_recv.at[mine], target
            ).wait_send()
            remote(
                fq, fgbuf.at[group, pl.ds(QUART * part, QUART)],
                fb_send.at[target], fb_recv.at[mine], target,
            ).wait_send()
            return carry

        lax.fori_loop(1, NB, drain, 0)


def local(query_in, key_in, value_in, short_taps, long_filters, skip_gain, cotangent):
    vmem = pl.BlockSpec(memory_space=pltpu.VMEM)
    dma = pltpu.SemaphoreType.DMA
    results = pl.pallas_call(
        kernel,
        out_shape=(
            jax.ShapeDtypeStruct((BLK, BLK), BF16),
            jax.ShapeDtypeStruct((3, BLK, BLK), BF16),
            jax.ShapeDtypeStruct((3, TAPS, BLK), F32),
            jax.ShapeDtypeStruct((1, BLK), F32),
            jax.ShapeDtypeStruct((NG, NB * BLK), F32),
        ),
        in_specs=[vmem] * 7,
        out_specs=(vmem,) * 5,
        scratch_shapes=[
            pltpu.VMEM((512, 512), BF16),
            pltpu.VMEM((NW, 16, BLK), BF16),
            pltpu.VMEM((NB, 16, BLK), BF16),
            pltpu.VMEM((NB + 1, BLK, BLK), BF16),
            pltpu.VMEM((TAPS, 16, BLK), F32),
            pltpu.VMEM((NB, 16, BLK), F32),
            pltpu.VMEM((NB, 8, BLK), F32),
            pltpu.VMEM((NB + 1, 8, BLK), F32),
            pltpu.VMEM((32, 8, BLK), F32),
            pltpu.VMEM((PAIRS + 32, 8, 2 * BLK), F32),
            pltpu.VMEM((PAIRS, 8, 2 * BLK), F32),
            pltpu.VMEM((2 * PAIRS, 8, 2 * BLK), F32),
            pltpu.VMEM((PAIRS, 8, 2 * BLK), F32),
            pltpu.VMEM((NB, 16, BLK), BF16),
            pltpu.VMEM((NW, 16, BLK), BF16),
            pltpu.VMEM((1, BLK), F32),
            pltpu.VMEM((NW, 1, BLK), F32),
            pltpu.VMEM((BLK, BLK), F32),
            pltpu.VMEM((NB + 1, 1, BLK), F32),
            pltpu.VMEM((4, QUART, 1, BLK), F32),
            pltpu.VMEM((QUART, 1, BLK), F32),
            pltpu.VMEM((NG, NB, 1, BLK), F32),
            dma((NW,)), dma((NB,)), dma((NB,)), dma((NW,)), dma((NB,)), dma((NW,)),
            dma((4,)), dma((4,)), dma((NB,)), dma((NW,)),
        ],
        compiler_params=pltpu.CompilerParams(collective_id=0, has_side_effects=True),
        name="hyena",
    )(query_in, key_in, value_in, cotangent, short_taps, long_filters, skip_gain.reshape(1, BLK))
    block_out, input_grads, tap_grads, skip_grad, filter_grad = results
    return block_out, input_grads, tap_grads, skip_grad.reshape(BLK), filter_grad


def solution(mesh):
    in_specs = (
        P("seq", "chan"),
        P("seq", "chan"),
        P("seq", "chan"),
        P(None, None, "chan"),
        P("chan", None),
        P("chan"),
        P("seq", "chan"),
    )
    out_specs = (
        P("seq", "chan"),
        P(None, "seq", "chan"),
        P(None, None, "chan"),
        P("chan"),
        P("chan", None),
    )
    return jax.shard_map(local, mesh=mesh, in_specs=in_specs, out_specs=out_specs, check_vma=False)
```

time: 1040 us -> 72.3 us (0.07)
  waiting for transfers between devices: 364 us -> 0 us
  local copies, waits for them, and re-layouts: 328 us -> 4.77 us
  blocking collectives: 206 us -> 0 us
  loops' own time: 72.3 us -> 0 us
  Pallas kernels: 0 us -> 66.7 us
  matrix products: 28.1 us -> 0 us
  other arithmetic: 17.6 us -> 0 us
  between operations: 14.5 us -> 0.65 us
    psum x1 -> x0, blocking collectives: 206 us -> none  [local(): lax.psum((lag_local, tap_local, skip_local), 'seq')]
    psum x1 -> x0, waiting for transfers between devices: 199 us -> none  [local(): lax.psum((lag_local, tap_local, skip_local), 'seq')]
    all_gather x2 -> x0, waiting for transfers between devices: 160 us -> none  [the longest x1 116 us: local(): shard_rows = lax.all_gather(gating, 'seq', axis=0, tiled=True)]
    dynamic_slice x145 -> x0, local copies, waits for them, and re-layouts: 95.2 us -> none  [the longest x96 91 us: local(): lax.scan(forward_visit_block, totals, (jnp.arange(piece_rows // step_rows...]
    another operation x147 -> x0, loops' own time: 72.3 us -> none  [the longest x1 32.8 us: local(): lax.scan(backward_visit_block, totals, (jnp.arange(piece_rows // backward...]
    reshape x48 -> x0, local copies, waits for them, and re-layouts: 67.3 us -> none  [lag_part(): skewed = skewed.reshape(groups, height, full_width - 1)]
    pallas_call x0 -> x1, Pallas kernels: none -> 66.7 us  [local(): pl.pallas_call(kernel, out_shape=(jax.ShapeDtypeStruct((BLK, BLK), BF16),...]
    squeeze x51 -> x0, local copies, waits for them, and re-layouts: 37.6 us -> none  [the longest x49 37.6 us: local(): lax.scan(forward_visit_block, totals, (jnp.arange(piece_rows // step_rows...]
  transfers between devices with their start and end apart: 5 -> 0, of which waited for: 4 -> 0; matrix products, arithmetic and copies ran while one was open for 4% -> 0% of each run, Pallas kernels for 0% -> 0%
where the time goes in v1:
time: 72.3 us; the launch traced here: 72.1 us
  Pallas kernels  66.7 us (92%)
  local copies, waits for them, and re-layouts  4.77 us (7%)
    pallas_call x1, Pallas kernels, local(): pl.pallas_call(kernel, out_shape=(jax.ShapeDtypeStruct((BLK, BLK), BF16),...  66.7 us
    unnamed x11, local copies, waits for them, and re-layouts  4.77 us

profile of v1, /device:TPU:56, one launch (start us, length us, event | category | flops | bytes accessed | tf_op | source)
XLA Modules:
  0.0 72.1 jit_solution(10351671838140687606)
XLA Ops:
  0.6 66.7 %hyena.1 = (bf16[128,128]{1,0:T(8,128)(2,1)}, bf16[3,128,128]{2,1,0:T(8,128)(2,1)}, f32[3,7,128]{2,1,0:T(8,128)}, f32[1,128]{1,0:T(1,128)}, f32[8,6144]{1,0:T(8,128)}) custom-call(bf16[128,128]{1,0:T(8,128)(2,1)} %q_ref.1, bf16[128,128]{1,0:T(8,128)(2,1)} %k_ref.1, bf16[128,128]{1,0:T(8,128)(2,1)} %v_ref.1, bf16[128,128]{1,0:T(8,128)(2,1)} %c_ref.1, ...), custom_call_target="tpu_custom_call" | custom-call | tf_op jit(solution)/shard_map/hyena/pallas_call | solution.py:417
  67.3 0.0 copy-start
  67.3 1.4 %copy.17 = bf16[128,128]{1,0:T(8,128)(2,1)} copy(bf16[128,128]{1,0:T(8,128)(2,1)} %get-tuple-element.20) | data formatting | bytes 65536
  68.7 0.0 copy-start.1
  68.7 1.6 %copy.18 = bf16[3,128,128]{2,1,0:T(8,128)(2,1)} copy(bf16[3,128,128]{2,1,0:T(8,128)(2,1)} %get-tuple-element.21) | data formatting | bytes 196608
  70.3 0.0 copy-done.1
  70.3 0.0 copy-start.2
  70.3 0.6 copy.19
  70.9 0.0 copy-done.2
  70.9 0.5 copy.20
  71.4 0.0 copy-done
  71.4 0.7 copy.21
Async XLA Ops:
  67.3 4.1 %copy-start = (f32[8,6144]{1,0:T(8,128)S(1)}, f32[8,6144]{1,0:T(8,128)}, u32[]{:S(2)}) copy-start(f32[8,6144]{1,0:T(8,128)} %get-tuple-element.24) | copy-start | bytes 589828
  68.7 1.6 %copy-start.1 = (f32[3,7,128]{2,1,0:T(8,128)S(1)}, f32[3,7,128]{2,1,0:T(8,128)}, u32[]{:S(2)}) copy-start(f32[3,7,128]{2,1,0:T(8,128)} %get-tuple-element.22) | copy-start | bytes 32260
  70.3 0.6 copy-start.2

commit v2 on v1

v2 whole, which is shorter than its diff:
```python
import math

import jax
import jax.numpy as jnp
from jax import lax
from jax.experimental import pallas as pl
from jax.experimental.pallas import tpu as pltpu
from jax.sharding import PartitionSpec as P

F32 = jnp.float32
BF16 = jnp.bfloat16
MESH = pl.DeviceIdType.MESH

BLK = 128
NB = 48
NW = 32
TAPS = 7
NG = 8
QUART = NB // 4
PAIRS = NB // 2


def iota(shape, dim):
    return lax.broadcasted_iota(jnp.int32, shape, dim)


def dot(a, b, dims=((1,), (0,))):
    return lax.dot_general(a, b, (dims, ((), ())), preferred_element_type=F32)


def half_turn(x):
    return pltpu.roll(x, 4, 0)


def remote(src, dst, send_sem, recv_sem, target):
    return pltpu.make_async_remote_copy(
        src_ref=src,
        dst_ref=dst,
        send_sem=send_sem,
        recv_sem=recv_sem,
        device_id={"seq": target},
        device_id_type=MESH,
    )


def wait_for(ref, sem):
    pltpu.make_async_copy(ref, ref, sem).wait()


def transposer():
    rho = iota((512, 1), 0)
    column = 128 * ((rho // 4) % 4) + 4 * (rho // 16) + rho % 4
    return jnp.where(iota((512, 512), 1) == column, 1.0, 0.0).astype(BF16)


def kernel(
    q_hbm, k_hbm, c_hbm, v_hbm, taps_hbm, filt_hbm, skip_hbm,
    back_hbm, small_hbm, fg_hbm,
    streams, taps_ref, filt_ref, skip_ref,
    perm, sendb, recvb, toep, tcol, conv_s, pb_s, r8_s, gg_s, z_s, y_s, yj_s,
    retb, retr, small, smallr, fbuf, frecv, fq, fgbuf,
    load_sem, out_sem, in_send, in_recv, ret_send, ret_recv, sm_send, sm_recv,
    fr_send, fr_recv, fb_send, fb_recv,
):
    me = lax.axis_index("seq")
    plane = me // 4
    part = me % 4
    tap_scale = 1.0 / math.sqrt(NB * BLK)
    lag_scale = 1.0 / math.sqrt(NB * BLK * 16)
    working = me < NW
    barrier = pltpu.get_barrier_semaphore()

    loads = [
        pltpu.make_async_copy(source, streams.at[r], load_sem.at[r])
        for r, source in enumerate((q_hbm, k_hbm, c_hbm, v_hbm))
    ]
    for load in loads:
        load.start()
    own_loads = [
        pltpu.make_async_copy(taps_hbm, taps_ref, load_sem.at[4]),
        pltpu.make_async_copy(filt_hbm, filt_ref, load_sem.at[5]),
        pltpu.make_async_copy(skip_hbm, skip_ref, load_sem.at[6]),
    ]

    @pl.when(working)
    def _greet():
        for load in own_loads:
            load.start()

        def greet(i, carry):
            pl.semaphore_signal(
                barrier, inc=1, device_id={"seq": lax.rem(me + i, NB)}, device_id_type=MESH
            )
            return carry

        lax.fori_loop(1, NB, greet, 0)

    perm[...] = transposer()
    for load in loads:
        load.wait()
    joined = jnp.concatenate([streams[r] for r in range(4)], axis=1)
    sendb[...] = dot(perm[...], joined, ((1,), (1,))).astype(BF16).reshape(NW, 16, BLK)

    lane = iota((16, BLK), 1)
    row = iota((16, BLK), 0)
    low_rows = iota((8, BLK), 0) < 4
    square_row = iota((BLK, BLK), 0)
    square_lane = iota((BLK, BLK), 1)
    identity = jnp.where(square_row == square_lane, 1.0, 0.0).astype(BF16)
    flip = jnp.where(square_row + square_lane == BLK - 1, 1.0, 0.0).astype(BF16)

    @pl.when(working)
    def _prepare():
        for load in own_loads:
            load.wait()

        own = lane == 4 * me + row % 4
        for j in range(TAPS):
            q_tap = jnp.broadcast_to(taps_ref[0, j : j + 1, :], (16, BLK))
            k_tap = jnp.broadcast_to(taps_ref[1, j : j + 1, :], (16, BLK))
            v_tap = jnp.broadcast_to(taps_ref[2, j : j + 1, :], (16, BLK))
            tap = jnp.where(row < 4, q_tap, jnp.where(row < 8, k_tap, v_tap))
            column = jnp.sum(jnp.where(own, tap, 0.0), axis=1, keepdims=True)
            column = jnp.broadcast_to(column, (16, BLK))
            unit = 1.0 if j == 0 else 0.0
            tcol[j] = jnp.where((row >= 8) & (row < 12), unit, column)
        skip_own = jnp.where(own, jnp.broadcast_to(skip_ref[...], (16, BLK)), 0.0)
        tcol[TAPS] = jnp.broadcast_to(jnp.sum(skip_own, axis=1, keepdims=True), (16, BLK))

        toep[0] = jnp.zeros((BLK, BLK), BF16)

        def build(n, previous):
            rows = filt_ref[:, pl.ds(pl.multiple_of(n * BLK, BLK), BLK)].astype(F32)
            line = jnp.sum(jnp.where(iota((NG, BLK), 0) == plane, rows, 0.0), axis=0, keepdims=True)
            turned = pltpu.roll(
                jnp.broadcast_to(line, (BLK, BLK)), 0, 1, stride=1, stride_axis=0
            )
            toep[n + 1] = jnp.where(square_lane >= square_row, turned, previous).astype(BF16)
            return turned

        lax.fori_loop(0, NB, build, jnp.zeros((BLK, BLK), F32), unroll=2)

        r8_s[PAIRS:] = jnp.zeros((32 - PAIRS, 8, BLK), F32)
        gg_s[:PAIRS] = jnp.zeros((PAIRS, 8, 2 * BLK), F32)
        gg_s[2 * PAIRS :] = jnp.zeros((32 - PAIRS, 8, 2 * BLK), F32)
        y_s[...] = jnp.zeros((2 * PAIRS, 8, 2 * BLK), F32)
        recvb[me] = sendb[me]
        pl.semaphore_wait(barrier, NW - 1)

    @pl.when(me >= NW)
    def _():
        pl.semaphore_wait(barrier, NW)

    for m in range(NW):
        @pl.when(m != me)
        def _(m=m):
            remote(sendb.at[m], recvb.at[me], in_send, in_recv.at[plane], m).start()

    @pl.when(working)
    def _work():
        skip_col = tcol[TAPS][:8]

        def short(z, carry):
            before, jm = carry

            @pl.when(z == plane)
            def _():
                wait_for(recvb.at[pl.ds(0, 3)], in_recv.at[z])

            @pl.when(z != plane)
            def _():
                wait_for(recvb.at[pl.ds(0, 4)], in_recv.at[z])

            for b4 in range(4):
                b = 4 * z + b4
                x = recvb[b].astype(F32)
                total = tcol[0] * x
                turned = []
                for j in range(1, TAPS):
                    t = pltpu.roll(x, j, 1)
                    total = total + tcol[j] * jnp.where(lane < j, before[j - 1], t)
                    turned.append(t)
                conv_s[b] = total
                pb_s[b] = (total[:8] * total[8:]).astype(BF16).astype(F32)
                before = tuple(turned)

            pb4 = pb_s[pl.ds(4 * z, 4)]
            pj4 = dot(pb4.reshape(32, BLK).astype(BF16), flip).reshape(4, 8, BLK)
            for half in range(2):
                e = 2 * z + half
                p0, p1 = pb4[2 * half], pb4[2 * half + 1]
                j0, j1 = pj4[2 * half], pj4[2 * half + 1]
                r8_s[e] = jnp.where(low_rows, p0, half_turn(p1))
                gg_s[PAIRS + e, :, :BLK] = jnp.where(low_rows, half_turn(j0), j1)
                gg_s[PAIRS + e, :, BLK:] = jnp.where(low_rows, half_turn(jm), j0)
                z_s[e, 4:, :BLK] = p0[4:]
                z_s[e, 4:, BLK:] = p1[4:]
                z_s[PAIRS - 1 - e, :4, :BLK] = j1[:4]
                z_s[PAIRS - 1 - e, :4, BLK:] = j0[:4]
                jm = j1
            return before, jm

        empty = tuple(jnp.zeros((16, BLK), F32) for _ in range(TAPS - 1))
        lax.fori_loop(0, NB // 4, short, (empty, jnp.zeros((8, BLK), F32)))

        r8_t = dot(identity, r8_s[...].reshape(256, BLK).astype(BF16), ((1,), (1,))).astype(BF16)
        inside = square_lane <= square_row

        def lags(f, previous):
            shifted = gg_s[pl.ds(PAIRS - f, 32)].reshape(256, 2 * BLK).astype(BF16)
            product = dot(r8_t, shifted)
            even = pltpu.roll(product[:, :BLK], 1, 1, stride=1, stride_axis=0)
            odd = pltpu.roll(product[:, BLK:], 1, 1, stride=1, stride_axis=0)
            fbuf[2 * f] = jnp.sum(jnp.where(inside, previous, even), axis=0, keepdims=True)
            fbuf[2 * f + 1] = jnp.sum(jnp.where(inside, even, odd), axis=0, keepdims=True)
            return odd

        last = lax.fori_loop(0, PAIRS, lags, jnp.zeros((BLK, BLK), F32), unroll=2)
        fbuf[NB] = jnp.sum(jnp.where(inside, last, 0.0), axis=0, keepdims=True)

        for i in range(1, 4):
            other = lax.rem(part + i, 4)
            remote(
                fbuf.at[pl.ds(1 + QUART * other, QUART)], frecv.at[part],
                fr_send, fr_recv, 4 * plane + other,
            ).start()
        frecv[part] = fbuf[pl.ds(1 + QUART * part, QUART)]

        z = z_s[...].reshape(PAIRS * 8, 2 * BLK).astype(BF16)

        def convolve(d, carry):
            t0, t1, t2 = toep[2 * d], toep[2 * d + 1], toep[2 * d + 2]
            weights = jnp.concatenate(
                [jnp.concatenate([t1, t2], axis=1), jnp.concatenate([t0, t1], axis=1)], axis=0
            )
            y_s[pl.ds(d, PAIRS)] += dot(z, weights).reshape(PAIRS, 8, 2 * BLK)
            return carry

        lax.fori_loop(0, PAIRS, convolve, 0, unroll=2)

        wait_for(frecv.at[pl.ds(0, 3)], fr_recv)
        fq[...] = lag_scale * ((frecv[0] + frecv[1]) + (frecv[2] + frecv[3]))

        for half in range(2):
            y = y_s[:PAIRS, :, half * BLK : (half + 1) * BLK].reshape(PAIRS * 8, BLK)
            high = y.astype(BF16)
            rest = (y - high.astype(F32)).astype(BF16)
            yj_s[:, :, half * BLK : (half + 1) * BLK] = (
                dot(high, flip) + dot(rest, flip)
            ).reshape(PAIRS, 8, BLK)

        def spread_lags(i, carry):
            remote(fq, fgbuf.at[me], fb_send, fb_recv, lax.rem(me + i, NB)).start()
            return carry

        lax.fori_loop(1, NB, spread_lags, 0)
        fgbuf[me] = fq[...]

        def finish(b, y, yj, after, sums, skip_sum):
            p = pb_s[b]
            u = half_turn(jnp.where(low_rows, yj, y) + skip_col * p)
            short_tile = conv_s[b]
            he = jnp.concatenate([short_tile[8:] * u, short_tile[:8] * u], axis=0)
            x = recvb[b].astype(F32)
            total = tcol[0] * he
            new_sums = [sums[0] + he * x]
            turned = []
            for j in range(1, TAPS):
                t = pltpu.roll(he, BLK - j, 1)
                s = jnp.where(lane < BLK - j, t, after[j - 1])
                total = total + tcol[j] * s
                new_sums.append(sums[j] + s * x)
                turned.append(t)
            retb[b] = total.astype(BF16)
            return tuple(turned), tuple(new_sums), skip_sum + p * half_turn(p)

        def send_plane(zp):
            for b4 in range(4):
                b = 4 * zp + b4

                @pl.when(b != me)
                def _(b=b):
                    remote(retb.at[b], retr.at[me], ret_send, ret_recv, b).start()

        def post(i, carry):
            after, sums, skip_sum = carry
            zp = NB // 4 - 1 - i
            for b4 in range(3, -1, -1):
                y_half = slice(BLK, None) if b4 % 2 else slice(0, BLK)
                j_half = slice(0, BLK) if b4 % 2 else slice(BLK, None)
                e = 2 * zp + b4 // 2
                after, sums, skip_sum = finish(
                    4 * zp + b4, y_s[e, :, y_half], yj_s[PAIRS - 1 - e, :, j_half],
                    after, sums, skip_sum,
                )

            @pl.when(i > 0)
            def _():
                send_plane(zp + 1)

            return after, sums, skip_sum

        start = (
            empty,
            tuple(jnp.zeros((16, BLK), F32) for _ in range(TAPS)),
            jnp.zeros((8, BLK), F32),
        )
        _, sums, skip_sum = lax.fori_loop(0, NB // 4, post, start)

        line = jnp.zeros((16, BLK), F32)
        for j in range(TAPS):
            line = line + jnp.where(
                lane == 16 * j + row, jnp.sum(sums[j], axis=1, keepdims=True), 0.0
            )
        skip_line = jnp.where(
            lane[:8] == 16 * TAPS + row[:8], jnp.sum(skip_sum, axis=1, keepdims=True), 0.0
        )
        small[...] = tap_scale * (
            jnp.sum(line, axis=0, keepdims=True) + jnp.sum(skip_line, axis=0, keepdims=True)
        )
        send_plane(0)

        def spread_small(i, carry):
            remote(small, smallr.at[me], sm_send, sm_recv, lax.rem(me + i, NB)).start()
            return carry

        lax.fori_loop(1, NB, spread_small, 0)
        retr[me] = retb[me]
        smallr[me] = small[...]

    outs = [
        pltpu.make_async_copy(fgbuf, fg_hbm, out_sem.at[0]),
        pltpu.make_async_copy(retr, back_hbm, out_sem.at[1]),
        pltpu.make_async_copy(smallr, small_hbm, out_sem.at[2]),
    ]
    for out, buffer, sem in zip(outs, (fgbuf, retr, smallr), (fb_recv, ret_recv, sm_recv)):
        @pl.when(working)
        def _(buffer=buffer, sem=sem):
            wait_for(buffer.at[pl.ds(0, NW - 1)], sem)

        @pl.when(me >= NW)
        def _(buffer=buffer, sem=sem):
            wait_for(buffer, sem)

        out.start()

    @pl.when(working)
    def _drain():
        wait_for(sendb.at[pl.ds(0, NW - 1)], in_send)
        wait_for(frecv.at[pl.ds(0, 3)], fr_send)
        wait_for(retb.at[pl.ds(0, NB - 1)], ret_send)

        def drain(i, carry):
            wait_for(fq, fb_send)
            wait_for(small, sm_send)
            return carry

        lax.fori_loop(1, NB, drain, 0)

    @pl.when(me >= NW)
    def _():
        wait_for(sendb, in_send)

    for out in outs:
        out.wait()


def assemble(
    back_hbm, small_hbm, fg_hbm,
    out_ref, ig_ref, tapg_ref, skipg_ref, fg_ref,
    backb, smallb, fgbuf, sm_s, sems,
):
    loads = [
        pltpu.make_async_copy(back_hbm, backb, sems.at[0]),
        pltpu.make_async_copy(small_hbm, smallb, sems.at[1]),
        pltpu.make_async_copy(fg_hbm, fgbuf, sems.at[2]),
    ]
    for load in loads:
        load.start()
    perm = transposer()
    loads[0].wait()
    back = dot(backb[...].reshape(512, BLK), perm, ((0,), (0,))).astype(BF16)
    ig_ref[0] = back[:, 0:128]
    ig_ref[1] = back[:, 128:256]
    out_ref[...] = back[:, 256:384]
    ig_ref[2] = back[:, 384:512]

    loads[1].wait()
    sm_s[...] = jnp.zeros((BLK, BLK), F32)
    for m in range(NW):
        sm_s[m : m + 1, :] = smallb[m]
    select = jnp.where(iota((BLK, BLK), 0) == iota((BLK, BLK), 1) // 4, 1.0, 0.0)
    spread = lax.dot_general(
        sm_s[...].T, select, (((1,), (0,)), ((), ())),
        precision=lax.Precision.HIGHEST, preferred_element_type=F32,
    ).reshape(8, 16, BLK)
    row3 = iota((8, 16, BLK), 1)
    channel = iota((8, 16, BLK), 2) % 4
    for stream, first in enumerate((0, 4, 12)):
        picked = jnp.sum(jnp.where(row3 == channel + first, spread, 0.0), axis=1)
        tapg_ref[stream] = picked[:TAPS]
        if stream == 0:
            skipg_ref[...] = picked[TAPS:]

    loads[2].wait()
    for part in range(4):
        def lay(n, carry, part=part):
            at = pl.ds(pl.multiple_of((QUART * part + n) * BLK, BLK), BLK)
            for g in range(NG):
                fg_ref[g : g + 1, at] = fgbuf[4 * g + part, n]
            return carry

        lax.fori_loop(0, QUART, lay, 0)


def local(query_in, key_in, value_in, short_taps, long_filters, skip_gain, cotangent):
    vmem = pl.BlockSpec(memory_space=pltpu.VMEM)
    anywhere = pl.BlockSpec(memory_space=pl.ANY)
    dma = pltpu.SemaphoreType.DMA
    raw = (
        jax.ShapeDtypeStruct((NW, 16, BLK), BF16),
        jax.ShapeDtypeStruct((NW, 1, BLK), F32),
        jax.ShapeDtypeStruct((NW, QUART, 1, BLK), F32),
    )
    back, small, lag_rows = pl.pallas_call(
        kernel,
        out_shape=raw,
        in_specs=[anywhere] * 7,
        out_specs=(anywhere,) * 3,
        scratch_shapes=[
            pltpu.VMEM((4, BLK, BLK), BF16),
            pltpu.VMEM((3, TAPS, BLK), F32),
            pltpu.VMEM((NG, NB * BLK), BF16),
            pltpu.VMEM((1, BLK), F32),
            pltpu.VMEM((512, 512), BF16),
            pltpu.VMEM((NW, 16, BLK), BF16),
            pltpu.VMEM((NB, 16, BLK), BF16),
            pltpu.VMEM((NB + 1, BLK, BLK), BF16),
            pltpu.VMEM((TAPS + 1, 16, BLK), F32),
            pltpu.VMEM((NB, 16, BLK), F32),
            pltpu.VMEM((NB, 8, BLK), F32),
            pltpu.VMEM((32, 8, BLK), F32),
            pltpu.VMEM((PAIRS + 32, 8, 2 * BLK), F32),
            pltpu.VMEM((PAIRS, 8, 2 * BLK), F32),
            pltpu.VMEM((2 * PAIRS, 8, 2 * BLK), F32),
            pltpu.VMEM((PAIRS, 8, 2 * BLK), F32),
            pltpu.VMEM((NB, 16, BLK), BF16),
            pltpu.VMEM((NW, 16, BLK), BF16),
            pltpu.VMEM((1, BLK), F32),
            pltpu.VMEM((NW, 1, BLK), F32),
            pltpu.VMEM((NB + 1, 1, BLK), F32),
            pltpu.VMEM((4, QUART, 1, BLK), F32),
            pltpu.VMEM((QUART, 1, BLK), F32),
            pltpu.VMEM((NW, QUART, 1, BLK), F32),
            dma((7,)), dma((3,)), dma(()), dma((NB // 4,)), dma(()), dma(()), dma(()), dma(()),
            dma(()), dma(()), dma(()), dma(()),
        ],
        compiler_params=pltpu.CompilerParams(collective_id=0, has_side_effects=True),
        name="hyena",
    )(query_in, key_in, cotangent, value_in, short_taps, long_filters, skip_gain.reshape(1, BLK))
    block_out, input_grads, tap_grads, skip_grad, filter_grad = pl.pallas_call(
        assemble,
        out_shape=(
            jax.ShapeDtypeStruct((BLK, BLK), BF16),
            jax.ShapeDtypeStruct((3, BLK, BLK), BF16),
            jax.ShapeDtypeStruct((3, TAPS, BLK), F32),
            jax.ShapeDtypeStruct((1, BLK), F32),
            jax.ShapeDtypeStruct((NG, NB * BLK), F32),
        ),
        in_specs=[anywhere] * 3,
        out_specs=(vmem,) * 5,
        scratch_shapes=[
            pltpu.VMEM((NW, 16, BLK), BF16),
            pltpu.VMEM((NW, 1, BLK), F32),
            pltpu.VMEM((NW, QUART, 1, BLK), F32),
            pltpu.VMEM((BLK, BLK), F32),
            dma((3,)),
        ],
        name="assemble",
    )(back, small, lag_rows)
    return block_out, input_grads, tap_grads, skip_grad.reshape(BLK), filter_grad


def solution(mesh):
    in_specs = (
        P("seq", "chan"),
        P("seq", "chan"),
        P("seq", "chan"),
        P(None, None, "chan"),
        P("chan", None),
        P("chan"),
        P("seq", "chan"),
    )
    out_specs = (
        P("seq", "chan"),
        P(None, "seq", "chan"),
        P(None, None, "chan"),
        P("chan"),
        P("chan", None),
    )
    return jax.shard_map(local, mesh=mesh, in_specs=in_specs, out_specs=out_specs, check_vma=False)
```

time: 72.3 us -> 60.8 us (0.84)
  Pallas kernels: 66.7 us -> 59.9 us
  local copies, waits for them, and re-layouts: 4.77 us -> 0 us
    pallas_call x1 -> x2, Pallas kernels: 66.7 us -> 59.9 us  [the longest x1 57.4 us: local(): pl.pallas_call(kernel, out_shape=raw, in_specs=[anywhere] * 7, out_specs=...]
    unnamed x11 -> x0, local copies, waits for them, and re-layouts: 4.77 us -> none
where the time goes in v2:
time: 60.8 us; the launch traced here: 60.6 us
  Pallas kernels  59.9 us (99%)
  between operations  0.64 us (1%)
    pallas_call x1, Pallas kernels, local(): pl.pallas_call(kernel, out_shape=raw, in_specs=[anywhere] * 7, out_specs=...  57.4 us
    pallas_call x1, Pallas kernels, local(): pl.pallas_call(assemble, out_shape=(jax.ShapeDtypeStruct((BLK, BLK), BF16...  2.54 us

profile of v2, /device:TPU:56, one launch (start us, length us, event | category | flops | bytes accessed | tf_op | source)
XLA Modules:
  0.0 60.6 jit_solution(5678272186639711032)
XLA Ops:
  0.6 57.4 %hyena.1 = (bf16[32,16,128]{2,1,0:T(8,128)(2,1)}, f32[32,1,128]{2,1,0:T(1,128)}, f32[32,12,1,128]{3,2,1,0:T(1,128)}) custom-call(bf16[128,128]{1,0:T(8,128)(2,1)} %q_hbm.1, bf16[128,128]{1,0:T(8,128)(2,1)} %k_hbm.1, bf16[128,128]{1,0:T(8,128)(2,1)} %c_hbm.1, bf16[128,128]{1,0:T(8,128)(2,1)} %v_hbm.1, f32[3,7,128]{2,1,0:T(8,128)} %taps_hbm.1, ...), custom_call_target="tpu_custom_call" | custom-call | tf_op jit(solution)/shard_map/hyena/pallas_call | solution.py:425
  58.0 2.5 %assemble.1 = (bf16[128,128]{1,0:T(8,128)(2,1)}, bf16[3,128,128]{2,1,0:T(8,128)(2,1)}, f32[3,7,128]{2,1,0:T(8,128)}, f32[1,128]{1,0:T(1,128)}, f32[8,6144]{1,0:T(8,128)}) custom-call(bf16[32,16,128]{2,1,0:T(8,128)(2,1)} %get-tuple-element.13.back_hbm, f32[32,1,128]{2,1,0:T(1,128)} %get-tuple-element.14.small_hbm, f32[32,12,1,128]{3,2,1,0:T(1,128)} %get-tuple-element.15.fg_hbm), custom_call_target="tpu_custom_call" | custom-call | tf_op jit(solution)/shard_map/assemble/pallas_call | solution.py:461

commit v3 on v2

--- a/solution.py
+++ b/solution.py
@@ -57,10 +57,10 @@
     q_hbm, k_hbm, c_hbm, v_hbm, taps_hbm, filt_hbm, skip_hbm,
     back_hbm, small_hbm, fg_hbm,
     streams, taps_ref, filt_ref, skip_ref,
-    perm, sendb, recvb, toep, tcol, conv_s, pb_s, r8_s, gg_s, z_s, y_s, yj_s,
+    perm, sendb, recvb, toep, tcol, conv_s, pb_s, r8_s, gg_s, ggb, z_s, zb, y_s, yj_s,
     retb, retr, small, smallr, fbuf, frecv, fq, fgbuf,
     load_sem, out_sem, in_send, in_recv, ret_send, ret_recv, sm_send, sm_recv,
-    fr_send, fr_recv, fb_send, fb_recv,
+    fr_send, fr_recv, fb_send, fb_recv, fx_send, fx_recv,
 ):
     me = lax.axis_index("seq")
     plane = me // 4
@@ -141,9 +141,7 @@
         lax.fori_loop(0, NB, build, jnp.zeros((BLK, BLK), F32), unroll=2)
 
         r8_s[PAIRS:] = jnp.zeros((32 - PAIRS, 8, BLK), F32)
-        gg_s[:PAIRS] = jnp.zeros((PAIRS, 8, 2 * BLK), F32)
-        gg_s[2 * PAIRS :] = jnp.zeros((32 - PAIRS, 8, 2 * BLK), F32)
-        y_s[...] = jnp.zeros((2 * PAIRS, 8, 2 * BLK), F32)
+        gg_s[PAIRS:] = jnp.zeros((42 - PAIRS, 8, 2 * BLK), F32)
         recvb[me] = sendb[me]
         pl.semaphore_wait(barrier, NW - 1)
 
@@ -190,9 +188,9 @@
                 e = 2 * z + half
                 p0, p1 = pb4[2 * half], pb4[2 * half + 1]
                 j0, j1 = pj4[2 * half], pj4[2 * half + 1]
-                r8_s[e] = jnp.where(low_rows, p0, half_turn(p1))
-                gg_s[PAIRS + e, :, :BLK] = jnp.where(low_rows, half_turn(j0), j1)
-                gg_s[PAIRS + e, :, BLK:] = jnp.where(low_rows, half_turn(jm), j0)
+                r8_s[PAIRS - 1 - e] = jnp.where(low_rows, p0, half_turn(p1))
+                gg_s[PAIRS - 1 - e, :, :BLK] = jnp.where(low_rows, half_turn(j0), j1)
+                gg_s[PAIRS - 1 - e, :, BLK:] = jnp.where(low_rows, half_turn(jm), j0)
                 z_s[e, 4:, :BLK] = p0[4:]
                 z_s[e, 4:, BLK:] = p1[4:]
                 z_s[PAIRS - 1 - e, :4, :BLK] = j1[:4]
@@ -206,73 +204,85 @@
         r8_t = dot(identity, r8_s[...].reshape(256, BLK).astype(BF16), ((1,), (1,))).astype(BF16)
         inside = square_lane <= square_row
 
-        def lags(f, previous):
-            shifted = gg_s[pl.ds(PAIRS - f, 32)].reshape(256, 2 * BLK).astype(BF16)
-            product = dot(r8_t, shifted)
-            even = pltpu.roll(product[:, :BLK], 1, 1, stride=1, stride_axis=0)
-            odd = pltpu.roll(product[:, BLK:], 1, 1, stride=1, stride_axis=0)
-            fbuf[2 * f] = jnp.sum(jnp.where(inside, previous, even), axis=0, keepdims=True)
-            fbuf[2 * f + 1] = jnp.sum(jnp.where(inside, even, odd), axis=0, keepdims=True)
-            return odd
-
-        last = lax.fori_loop(0, PAIRS, lags, jnp.zeros((BLK, BLK), F32), unroll=2)
-        fbuf[NB] = jnp.sum(jnp.where(inside, last, 0.0), axis=0, keepdims=True)
+        for odd in range(2):
+            ggb[odd] = gg_s[odd : odd + 40].reshape(320, 2 * BLK).astype(BF16)
+
+        def fold(x):
+            return jnp.sum(x.reshape(BLK // 8, 8, BLK), axis=0)
+
+        within = None
+        for f in range(PAIRS):
+            depth = 256 if f < 8 else 128
+            first = 8 * (f - f % 2)
+            product = dot(r8_t[:, :depth], ggb[f % 2, first : first + depth, :])
+            for half in range(2):
+                n = 2 * f + half
+                turned = pltpu.roll(
+                    product[:, half * BLK : (half + 1) * BLK], 1, 1, stride=1, stride_axis=0
+                )
+                everything = fold(turned)
+                next_within = fold(jnp.where(inside, turned, 0.0))
+                if n > 0:
+                    fbuf[n - 1] = jnp.sum(
+                        within + (everything - next_within), axis=0, keepdims=True
+                    )
+                within = next_within
+        fbuf[NB - 1] = jnp.sum(within, axis=0, keepdims=True)
 
         for i in range(1, 4):
             other = lax.rem(part + i, 4)
             remote(
-                fbuf.at[pl.ds(1 + QUART * other, QUART)], frecv.at[part],
+                fbuf.at[pl.ds(QUART * other, QUART)], frecv.at[part],
                 fr_send, fr_recv, 4 * plane + other,
             ).start()
-        frecv[part] = fbuf[pl.ds(1 + QUART * part, QUART)]
-
-        z = z_s[...].reshape(PAIRS * 8, 2 * BLK).astype(BF16)
-
-        def convolve(d, carry):
+        frecv[part] = fbuf[pl.ds(QUART * part, QUART)]
+
+        zb[...] = z_s[...].reshape(PAIRS * 8, 2 * BLK).astype(BF16)
+        for d in range(PAIRS):
             t0, t1, t2 = toep[2 * d], toep[2 * d + 1], toep[2 * d + 2]
             weights = jnp.concatenate(
                 [jnp.concatenate([t1, t2], axis=1), jnp.concatenate([t0, t1], axis=1)], axis=0
             )
-            y_s[pl.ds(d, PAIRS)] += dot(z, weights).reshape(PAIRS, 8, 2 * BLK)
-            return carry
-
-        lax.fori_loop(0, PAIRS, convolve, 0, unroll=2)
+            term = dot(zb[: 8 * (PAIRS - d), :], weights).reshape(PAIRS - d, 8, 2 * BLK)
+            if d == 0:
+                y_s[...] = term
+            else:
+                y_s[d:] += term
 
         wait_for(frecv.at[pl.ds(0, 3)], fr_recv)
         fq[...] = lag_scale * ((frecv[0] + frecv[1]) + (frecv[2] + frecv[3]))
 
         for half in range(2):
-            y = y_s[:PAIRS, :, half * BLK : (half + 1) * BLK].reshape(PAIRS * 8, BLK)
+            y = y_s[:, :, half * BLK : (half + 1) * BLK].reshape(PAIRS * 8, BLK)
             high = y.astype(BF16)
             rest = (y - high.astype(F32)).astype(BF16)
             yj_s[:, :, half * BLK : (half + 1) * BLK] = (
                 dot(high, flip) + dot(rest, flip)
             ).reshape(PAIRS, 8, BLK)
 
-        def spread_lags(i, carry):
-            remote(fq, fgbuf.at[me], fb_send, fb_recv, lax.rem(me + i, NB)).start()
-            return carry
-
-        lax.fori_loop(1, NB, spread_lags, 0)
-        fgbuf[me] = fq[...]
-
-        def finish(b, y, yj, after, sums, skip_sum):
+        for zp in range(NB // 4):
+            @pl.when(zp != plane)
+            def _(zp=zp):
+                remote(fq, fgbuf.at[part, plane], fb_send, fb_recv, 4 * zp + part).start()
+
+        fgbuf[part, plane] = fq[...]
+
+        def gates(b, y, yj):
             p = pb_s[b]
             u = half_turn(jnp.where(low_rows, yj, y) + skip_col * p)
             short_tile = conv_s[b]
             he = jnp.concatenate([short_tile[8:] * u, short_tile[:8] * u], axis=0)
-            x = recvb[b].astype(F32)
+            turned = tuple(pltpu.roll(he, BLK - j, 1) for j in range(1, TAPS))
+            return he, turned, p * half_turn(p)
+
+        def finish(he, turned, x, following, sums):
             total = tcol[0] * he
             new_sums = [sums[0] + he * x]
-            turned = []
             for j in range(1, TAPS):
-                t = pltpu.roll(he, BLK - j, 1)
-                s = jnp.where(lane < BLK - j, t, after[j - 1])
+                s = jnp.where(lane < BLK - j, turned[j - 1], following[j - 1])
                 total = total + tcol[j] * s
                 new_sums.append(sums[j] + s * x)
-                turned.append(t)
-            retb[b] = total.astype(BF16)
-            return tuple(turned), tuple(new_sums), skip_sum + p * half_turn(p)
+            return total.astype(BF16), tuple(new_sums)
 
         def send_plane(zp):
             for b4 in range(4):
@@ -280,32 +290,32 @@
 
                 @pl.when(b != me)
                 def _(b=b):
-                    remote(retb.at[b], retr.at[me], ret_send, ret_recv, b).start()
-
-        def post(i, carry):
-            after, sums, skip_sum = carry
-            zp = NB // 4 - 1 - i
-            for b4 in range(3, -1, -1):
+                    remote(retb.at[b + 1], retr.at[me], ret_send, ret_recv, b).start()
+
+        def post(zp, carry):
+            he, turned, x, sums, skip_sum = carry
+            for b4 in range(4):
+                b = 4 * zp + b4
                 y_half = slice(BLK, None) if b4 % 2 else slice(0, BLK)
                 j_half = slice(0, BLK) if b4 % 2 else slice(BLK, None)
                 e = 2 * zp + b4 // 2
-                after, sums, skip_sum = finish(
-                    4 * zp + b4, y_s[e, :, y_half], yj_s[PAIRS - 1 - e, :, j_half],
-                    after, sums, skip_sum,
+                new_he, following, skip_term = gates(
+                    b, y_s[e, :, y_half], yj_s[PAIRS - 1 - e, :, j_half]
                 )
-
-            @pl.when(i > 0)
+                retb[b], sums = finish(he, turned, x, following, sums)
+                he, turned, x = new_he, following, recvb[b].astype(F32)
+                skip_sum = skip_sum + skip_term
+
+            @pl.when((zp > 0) & (zp < 7))
             def _():
-                send_plane(zp + 1)
-
-            return after, sums, skip_sum
-
-        start = (
-            empty,
-            tuple(jnp.zeros((16, BLK), F32) for _ in range(TAPS)),
-            jnp.zeros((8, BLK), F32),
-        )
-        _, sums, skip_sum = lax.fori_loop(0, NB // 4, post, start)
+                send_plane(zp - 1)
+
+            return he, turned, x, sums, skip_sum
+
+        zero = jnp.zeros((16, BLK), F32)
+        start = (zero, empty, zero, (zero,) * TAPS, jnp.zeros((8, BLK), F32))
+        he, turned, x, sums, skip_sum = lax.fori_loop(0, NB // 4, post, start)
+        retb[NB], sums = finish(he, turned, x, empty, sums)
 
         line = jnp.zeros((16, BLK), F32)
         for j in range(TAPS):
@@ -318,22 +328,40 @@
         small[...] = tap_scale * (
             jnp.sum(line, axis=0, keepdims=True) + jnp.sum(skip_line, axis=0, keepdims=True)
         )
-        send_plane(0)
+        send_plane(6)
 
         def spread_small(i, carry):
-            remote(small, smallr.at[me], sm_send, sm_recv, lax.rem(me + i, NB)).start()
+            @pl.when(i != me)
+            def _():
+                remote(small, smallr.at[me], sm_send, sm_recv, i).start()
+
             return carry
 
-        lax.fori_loop(1, NB, spread_small, 0)
-        retr[me] = retb[me]
+        lax.fori_loop(0, NB // 2, spread_small, 0)
+        for zp in range(7, NB // 4):
+            send_plane(zp)
+        lax.fori_loop(NB // 2, NB, spread_small, 0)
+        retr[me] = retb[me + 1]
         smallr[me] = small[...]
 
+    @pl.when(working)
+    def _():
+        wait_for(fgbuf.at[0, pl.ds(0, NG - 1)], fb_recv)
+
+    @pl.when(me >= NW)
+    def _():
+        wait_for(fgbuf.at[0], fb_recv)
+
+    for i in range(1, 4):
+        other = lax.rem(part + i, 4)
+        remote(fgbuf.at[part], fgbuf.at[part], fx_send, fx_recv, 4 * plane + other).start()
+
     outs = [
-        pltpu.make_async_copy(fgbuf, fg_hbm, out_sem.at[0]),
-        pltpu.make_async_copy(retr, back_hbm, out_sem.at[1]),
-        pltpu.make_async_copy(smallr, small_hbm, out_sem.at[2]),
+        pltpu.make_async_copy(retr, back_hbm, out_sem.at[0]),
+        pltpu.make_async_copy(smallr, small_hbm, out_sem.at[1]),
+        pltpu.make_async_copy(fgbuf, fg_hbm, out_sem.at[2]),
     ]
-    for out, buffer, sem in zip(outs, (fgbuf, retr, smallr), (fb_recv, ret_recv, sm_recv)):
+    for out, buffer, sem in zip(outs[:2], (retr, smallr), (ret_recv, sm_recv)):
         @pl.when(working)
         def _(buffer=buffer, sem=sem):
             wait_for(buffer.at[pl.ds(0, NW - 1)], sem)
@@ -343,24 +371,23 @@
             wait_for(buffer, sem)
 
         out.start()
+    wait_for(fgbuf.at[pl.ds(0, 3)], fx_recv)
+    outs[2].start()
 
     @pl.when(working)
     def _drain():
         wait_for(sendb.at[pl.ds(0, NW - 1)], in_send)
         wait_for(frecv.at[pl.ds(0, 3)], fr_send)
         wait_for(retb.at[pl.ds(0, NB - 1)], ret_send)
-
-        def drain(i, carry):
-            wait_for(fq, fb_send)
-            wait_for(small, sm_send)
-            return carry
-
-        lax.fori_loop(1, NB, drain, 0)
+        wait_for(fbuf.at[pl.ds(0, NB - 1)], sm_send)
+        wait_for(fgbuf.at[0], fb_send)
+        wait_for(fgbuf.at[0, pl.ds(0, 3)], fb_send)
 
     @pl.when(me >= NW)
     def _():
         wait_for(sendb, in_send)
 
+    wait_for(fgbuf.at[pl.ds(0, 3)], fx_send)
     for out in outs:
         out.wait()
 
@@ -407,7 +434,7 @@
         def lay(n, carry, part=part):
             at = pl.ds(pl.multiple_of((QUART * part + n) * BLK, BLK), BLK)
             for g in range(NG):
-                fg_ref[g : g + 1, at] = fgbuf[4 * g + part, n]
+                fg_ref[g : g + 1, at] = fgbuf[part, g, n]
             return carry
 
         lax.fori_loop(0, QUART, lay, 0)
@@ -420,7 +447,7 @@
     raw = (
         jax.ShapeDtypeStruct((NW, 16, BLK), BF16),
         jax.ShapeDtypeStruct((NW, 1, BLK), F32),
-        jax.ShapeDtypeStruct((NW, QUART, 1, BLK), F32),
+        jax.ShapeDtypeStruct((4, NG, QUART, 1, BLK), F32),
     )
     back, small, lag_rows = pl.pallas_call(
         kernel,
@@ -440,20 +467,22 @@
             pltpu.VMEM((NB, 16, BLK), F32),
             pltpu.VMEM((NB, 8, BLK), F32),
             pltpu.VMEM((32, 8, BLK), F32),
-            pltpu.VMEM((PAIRS + 32, 8, 2 * BLK), F32),
+            pltpu.VMEM((42, 8, 2 * BLK), F32),
+            pltpu.VMEM((2, 320, 2 * BLK), BF16),
             pltpu.VMEM((PAIRS, 8, 2 * BLK), F32),
-            pltpu.VMEM((2 * PAIRS, 8, 2 * BLK), F32),
+            pltpu.VMEM((PAIRS * 8, 2 * BLK), BF16),
             pltpu.VMEM((PAIRS, 8, 2 * BLK), F32),
-            pltpu.VMEM((NB, 16, BLK), BF16),
+            pltpu.VMEM((PAIRS, 8, 2 * BLK), F32),
+            pltpu.VMEM((NB + 1, 16, BLK), BF16),
             pltpu.VMEM((NW, 16, BLK), BF16),
             pltpu.VMEM((1, BLK), F32),
             pltpu.VMEM((NW, 1, BLK), F32),
-            pltpu.VMEM((NB + 1, 1, BLK), F32),
+            pltpu.VMEM((NB, 1, BLK), F32),
             pltpu.VMEM((4, QUART, 1, BLK), F32),
             pltpu.VMEM((QUART, 1, BLK), F32),
-            pltpu.VMEM((NW, QUART, 1, BLK), F32),
+            pltpu.VMEM((4, NG, QUART, 1, BLK), F32),
             dma((7,)), dma((3,)), dma(()), dma((NB // 4,)), dma(()), dma(()), dma(()), dma(()),
-            dma(()), dma(()), dma(()), dma(()),
+            dma(()), dma(()), dma(()), dma(()), dma(()), dma(()),
         ],
         compiler_params=pltpu.CompilerParams(collective_id=0, has_side_effects=True),
         name="hyena",
@@ -472,7 +501,7 @@
         scratch_shapes=[
             pltpu.VMEM((NW, 16, BLK), BF16),
             pltpu.VMEM((NW, 1, BLK), F32),
-            pltpu.VMEM((NW, QUART, 1, BLK), F32),
+            pltpu.VMEM((4, NG, QUART, 1, BLK), F32),
             pltpu.VMEM((BLK, BLK), F32),
             dma((3,)),
         ],

time: 60.8 us -> 51.2 us (0.84)
  Pallas kernels: 59.9 us -> 50.3 us
    pallas_call x1, Pallas kernels: 57.4 us -> 47.8 us  [local(): pl.pallas_call(kernel, out_shape=raw, in_specs=[anywhere] * 7, out_specs=...]
where the time goes in v3:
time: 51.2 us; the launch traced here: 51 us
  Pallas kernels  50.3 us (98%)
  between operations  0.64 us (1%)
    pallas_call x1, Pallas kernels, local(): pl.pallas_call(kernel, out_shape=raw, in_specs=[anywhere] * 7, out_specs=...  47.8 us
    pallas_call x1, Pallas kernels, local(): pl.pallas_call(assemble, out_shape=(jax.ShapeDtypeStruct((BLK, BLK), BF16...  2.54 us

profile of v3, /device:TPU:56, one launch (start us, length us, event | category | flops | bytes accessed | tf_op | source)
XLA Modules:
  0.0 51.0 jit_solution(8217861612143310667)
XLA Ops:
  0.6 47.8 %hyena.1 = (bf16[32,16,128]{2,1,0:T(8,128)(2,1)}, f32[32,1,128]{2,1,0:T(1,128)}, f32[4,8,12,1,128]{4,3,2,1,0:T(1,128)}) custom-call(bf16[128,128]{1,0:T(8,128)(2,1)} %q_hbm.1, bf16[128,128]{1,0:T(8,128)(2,1)} %k_hbm.1, bf16[128,128]{1,0:T(8,128)(2,1)} %c_hbm.1, bf16[128,128]{1,0:T(8,128)(2,1)} %v_hbm.1, f32[3,7,128]{2,1,0:T(8,128)} %taps_hbm.1, ...), custom_call_target="tpu_custom_call" | custom-call | tf_op jit(solution)/shard_map/hyena/pallas_call | solution.py:452
  48.4 2.5 %assemble.1 = (bf16[128,128]{1,0:T(8,128)(2,1)}, bf16[3,128,128]{2,1,0:T(8,128)(2,1)}, f32[3,7,128]{2,1,0:T(8,128)}, f32[1,128]{1,0:T(1,128)}, f32[8,6144]{1,0:T(8,128)}) custom-call(bf16[32,16,128]{2,1,0:T(8,128)(2,1)} %get-tuple-element.13.back_hbm, f32[32,1,128]{2,1,0:T(1,128)} %get-tuple-element.14.small_hbm, f32[4,8,12,1,128]{4,3,2,1,0:T(1,128)} %get-tuple-element.15.fg_hbm), custom_call_target="tpu_custom_call" | custom-call | tf_op jit(solution)/shard_map/assemble/pallas_call | solution.py:490

commit v4 on v3

--- a/solution.py
+++ b/solution.py
@@ -60,7 +60,7 @@
     perm, sendb, recvb, toep, tcol, conv_s, pb_s, r8_s, gg_s, ggb, z_s, zb, y_s, yj_s,
     retb, retr, small, smallr, fbuf, frecv, fq, fgbuf,
     load_sem, out_sem, in_send, in_recv, ret_send, ret_recv, sm_send, sm_recv,
-    fr_send, fr_recv, fb_send, fb_recv, fx_send, fx_recv,
+    fr_send, fr_recv, fb_send, fb_recv, fx_send, fx_recv, ready,
 ):
     me = lax.axis_index("seq")
     plane = me // 4
@@ -88,12 +88,13 @@
             load.start()
 
         def greet(i, carry):
-            pl.semaphore_signal(
-                barrier, inc=1, device_id={"seq": lax.rem(me + i, NB)}, device_id_type=MESH
-            )
+            @pl.when(i != me)
+            def _():
+                pl.semaphore_signal(barrier, inc=1, device_id={"seq": i}, device_id_type=MESH)
+
             return carry
 
-        lax.fori_loop(1, NB, greet, 0)
+        lax.fori_loop(4 * plane, NB, greet, 0)
 
     perm[...] = transposer()
     for load in loads:
@@ -108,6 +109,33 @@
     square_lane = iota((BLK, BLK), 1)
     identity = jnp.where(square_row == square_lane, 1.0, 0.0).astype(BF16)
     flip = jnp.where(square_row + square_lane == BLK - 1, 1.0, 0.0).astype(BF16)
+
+    def send_in(zp):
+        for m in range(4 * zp, 4 * zp + 4):
+            @pl.when(m != me)
+            def _(m=m):
+                remote(sendb.at[m], recvb.at[me], in_send, in_recv.at[plane], m).start()
+
+    @pl.when(working)
+    def _():
+        pl.semaphore_wait(barrier, 4 * plane + 3)
+
+        def tell(i, carry):
+            pl.semaphore_signal(
+                ready.at[plane], inc=1, device_id={"seq": i}, device_id_type=MESH
+            )
+            return carry
+
+        lax.fori_loop(0, 4 * plane, tell, 0)
+
+    @pl.when(me >= NW)
+    def _():
+        pl.semaphore_wait(barrier, NW)
+
+    for zp in range(NW // 4):
+        @pl.when(zp <= plane)
+        def _(zp=zp):
+            send_in(zp)
 
     @pl.when(working)
     def _prepare():
@@ -143,16 +171,12 @@
         r8_s[PAIRS:] = jnp.zeros((32 - PAIRS, 8, BLK), F32)
         gg_s[PAIRS:] = jnp.zeros((42 - PAIRS, 8, 2 * BLK), F32)
         recvb[me] = sendb[me]
-        pl.semaphore_wait(barrier, NW - 1)
-
-    @pl.when(me >= NW)
-    def _():
-        pl.semaphore_wait(barrier, NW)
-
-    for m in range(NW):
-        @pl.when(m != me)
-        def _(m=m):
-            remote(sendb.at[m], recvb.at[me], in_send, in_recv.at[plane], m).start()
+
+    for zp in range(1, NW // 4):
+        @pl.when(zp > plane)
+        def _(zp=zp):
+            pl.semaphore_wait(ready.at[zp], 4)
+            send_in(zp)
 
     @pl.when(working)
     def _work():
@@ -483,6 +507,7 @@
             pltpu.VMEM((4, NG, QUART, 1, BLK), F32),
             dma((7,)), dma((3,)), dma(()), dma((NB // 4,)), dma(()), dma(()), dma(()), dma(()),
             dma(()), dma(()), dma(()), dma(()), dma(()), dma(()),
+            pltpu.SemaphoreType.REGULAR((NW // 4,)),
         ],
         compiler_params=pltpu.CompilerParams(collective_id=0, has_side_effects=True),
         name="hyena",

time: 51.2 us -> 50 us (0.977)
  the two profiles are of different devices: /device:TPU:56 before, /device:TPU:4 now
where the time goes in v4:
time: 50 us; the launch traced here: 49.8 us
  Pallas kernels  49.2 us (98%)
  between operations  0.64 us (1%)
    pallas_call x1, Pallas kernels, local(): pl.pallas_call(kernel, out_shape=raw, in_specs=[anywhere] * 7, out_specs=...  46.6 us
    pallas_call x1, Pallas kernels, local(): pl.pallas_call(assemble, out_shape=(jax.ShapeDtypeStruct((BLK, BLK), BF16...  2.54 us

profile of v4, /device:TPU:4, one launch (start us, length us, event | category | flops | bytes accessed | tf_op | source)
XLA Modules:
  0.0 49.8 jit_solution(17044061977263854265)
XLA Ops:
  0.6 46.6 %hyena.1 = (bf16[32,16,128]{2,1,0:T(8,128)(2,1)}, f32[32,1,128]{2,1,0:T(1,128)}, f32[4,8,12,1,128]{4,3,2,1,0:T(1,128)}) custom-call(bf16[128,128]{1,0:T(8,128)(2,1)} %q_hbm.1, bf16[128,128]{1,0:T(8,128)(2,1)} %k_hbm.1, bf16[128,128]{1,0:T(8,128)(2,1)} %c_hbm.1, bf16[128,128]{1,0:T(8,128)(2,1)} %v_hbm.1, f32[3,7,128]{2,1,0:T(8,128)} %taps_hbm.1, ...), custom_call_target="tpu_custom_call" | custom-call | tf_op jit(solution)/shard_map/hyena/pallas_call | solution.py:476
  47.3 2.5 %assemble.1 = (bf16[128,128]{1,0:T(8,128)(2,1)}, bf16[3,128,128]{2,1,0:T(8,128)(2,1)}, f32[3,7,128]{2,1,0:T(8,128)}, f32[1,128]{1,0:T(1,128)}, f32[8,6144]{1,0:T(8,128)}) custom-call(bf16[32,16,128]{2,1,0:T(8,128)(2,1)} %get-tuple-element.13.back_hbm, f32[32,1,128]{2,1,0:T(1,128)} %get-tuple-element.14.small_hbm, f32[4,8,12,1,128]{4,3,2,1,0:T(1,128)} %get-tuple-element.15.fg_hbm), custom_call_target="tpu_custom_call" | custom-call | tf_op jit(solution)/shard_map/assemble/pallas_call | solution.py:515

commit v5 on v4

--- a/solution.py
+++ b/solution.py
@@ -58,7 +58,7 @@
     back_hbm, small_hbm, fg_hbm,
     streams, taps_ref, filt_ref, skip_ref,
     perm, sendb, recvb, toep, tcol, conv_s, pb_s, r8_s, gg_s, ggb, z_s, zb, y_s, yj_s,
-    retb, retr, small, smallr, fbuf, frecv, fq, fgbuf,
+    retb, retr, small, smallr, fbuf, frecv, fqf, fq, fgbuf,
     load_sem, out_sem, in_send, in_recv, ret_send, ret_recv, sm_send, sm_recv,
     fr_send, fr_recv, fb_send, fb_recv, fx_send, fx_recv, ready,
 ):
@@ -177,6 +177,11 @@
         def _(zp=zp):
             pl.semaphore_wait(ready.at[zp], 4)
             send_in(zp)
+
+    def forward_lags():
+        for i in range(1, 4):
+            other = lax.rem(part + i, 4)
+            remote(fgbuf.at[part], fgbuf.at[part], fx_send, fx_recv, 4 * plane + other).start()
 
     @pl.when(working)
     def _work():
@@ -274,7 +279,12 @@
                 y_s[d:] += term
 
         wait_for(frecv.at[pl.ds(0, 3)], fr_recv)
-        fq[...] = lag_scale * ((frecv[0] + frecv[1]) + (frecv[2] + frecv[3]))
+        for n in range(QUART):
+            fqf[n : n + 1, :] = lag_scale * (
+                (frecv[0, n] + frecv[1, n]) + (frecv[2, n] + frecv[3, n])
+            )
+        fqf[QUART:, :] = jnp.zeros((16 - QUART, BLK), F32)
+        fq[...] = fqf[...].astype(BF16)
 
         for half in range(2):
             y = y_s[:, :, half * BLK : (half + 1) * BLK].reshape(PAIRS * 8, BLK)
@@ -362,23 +372,18 @@
             return carry
 
         lax.fori_loop(0, NB // 2, spread_small, 0)
+        wait_for(fgbuf.at[0, pl.ds(0, NG - 1)], fb_recv)
+        forward_lags()
         for zp in range(7, NB // 4):
             send_plane(zp)
         lax.fori_loop(NB // 2, NB, spread_small, 0)
         retr[me] = retb[me + 1]
         smallr[me] = small[...]
 
-    @pl.when(working)
-    def _():
-        wait_for(fgbuf.at[0, pl.ds(0, NG - 1)], fb_recv)
-
     @pl.when(me >= NW)
     def _():
         wait_for(fgbuf.at[0], fb_recv)
-
-    for i in range(1, 4):
-        other = lax.rem(part + i, 4)
-        remote(fgbuf.at[part], fgbuf.at[part], fx_send, fx_recv, 4 * plane + other).start()
+        forward_lags()
 
     outs = [
         pltpu.make_async_copy(retr, back_hbm, out_sem.at[0]),
@@ -419,7 +424,7 @@
 def assemble(
     back_hbm, small_hbm, fg_hbm,
     out_ref, ig_ref, tapg_ref, skipg_ref, fg_ref,
-    backb, smallb, fgbuf, sm_s, sems,
+    backb, smallb, fgbuf, fg_s, sm_s, sems,
 ):
     loads = [
         pltpu.make_async_copy(back_hbm, backb, sems.at[0]),
@@ -454,11 +459,12 @@
             skipg_ref[...] = picked[TAPS:]
 
     loads[2].wait()
+    fg_s[...] = fgbuf[...].astype(F32)
     for part in range(4):
         def lay(n, carry, part=part):
             at = pl.ds(pl.multiple_of((QUART * part + n) * BLK, BLK), BLK)
             for g in range(NG):
-                fg_ref[g : g + 1, at] = fgbuf[part, g, n]
+                fg_ref[g : g + 1, at] = fg_s[part, g, pl.ds(n, 1), :]
             return carry
 
         lax.fori_loop(0, QUART, lay, 0)
@@ -471,12 +477,12 @@
     raw = (
         jax.ShapeDtypeStruct((NW, 16, BLK), BF16),
         jax.ShapeDtypeStruct((NW, 1, BLK), F32),
-        jax.ShapeDtypeStruct((4, NG, QUART, 1, BLK), F32),
+        jax.ShapeDtypeStruct((4, NG, 16, BLK), BF16),
     )
     back, small, lag_rows = pl.pallas_call(
         kernel,
         out_shape=raw,
-        in_specs=[anywhere] * 7,
+        in_specs=[pl.BlockSpec(memory_space=pltpu.HBM)] * 7,
         out_specs=(anywhere,) * 3,
         scratch_shapes=[
             pltpu.VMEM((4, BLK, BLK), BF16),
@@ -503,15 +509,24 @@
             pltpu.VMEM((NW, 1, BLK), F32),
             pltpu.VMEM((NB, 1, BLK), F32),
             pltpu.VMEM((4, QUART, 1, BLK), F32),
-            pltpu.VMEM((QUART, 1, BLK), F32),
-            pltpu.VMEM((4, NG, QUART, 1, BLK), F32),
+            pltpu.VMEM((16, BLK), F32),
+            pltpu.VMEM((16, BLK), BF16),
+            pltpu.VMEM((4, NG, 16, BLK), BF16),
             dma((7,)), dma((3,)), dma(()), dma((NB // 4,)), dma(()), dma(()), dma(()), dma(()),
             dma(()), dma(()), dma(()), dma(()), dma(()), dma(()),
             pltpu.SemaphoreType.REGULAR((NW // 4,)),
         ],
-        compiler_params=pltpu.CompilerParams(collective_id=0, has_side_effects=True),
+        compiler_params=pltpu.CompilerParams(
+            collective_id=0, has_side_effects=True, vmem_limit_bytes=24 << 20
+        ),
         name="hyena",
-    )(query_in, key_in, cotangent, value_in, short_taps, long_filters, skip_gain.reshape(1, BLK))
+    )(*(
+        pltpu.with_memory_space_constraint(x, pltpu.HBM)
+        for x in (
+            query_in, key_in, cotangent, value_in, short_taps, long_filters,
+            skip_gain.reshape(1, BLK),
+        )
+    ))
     block_out, input_grads, tap_grads, skip_grad, filter_grad = pl.pallas_call(
         assemble,
         out_shape=(
@@ -526,10 +541,12 @@
         scratch_shapes=[
             pltpu.VMEM((NW, 16, BLK), BF16),
             pltpu.VMEM((NW, 1, BLK), F32),
-            pltpu.VMEM((4, NG, QUART, 1, BLK), F32),
+            pltpu.VMEM((4, NG, 16, BLK), BF16),
+            pltpu.VMEM((4, NG, 16, BLK), F32),
             pltpu.VMEM((BLK, BLK), F32),
             dma((3,)),
         ],
+        compiler_params=pltpu.CompilerParams(vmem_limit_bytes=8 << 20),
         name="assemble",
     )(back, small, lag_rows)
     return block_out, input_grads, tap_grads, skip_grad.reshape(BLK), filter_grad

time: 50 us -> 49 us (0.980)
  the two profiles are of different devices: /device:TPU:4 before, /device:TPU:2 now
where the time goes in v5:
time: 49 us; the launch traced here: 48.8 us
  Pallas kernels  48.2 us (98%)
  between operations  0.64 us (1%)
    pallas_call x1, Pallas kernels, local(): pl.pallas_call(kernel, out_shape=raw, in_specs=[pl.BlockSpec(memory_space...  46 us
    pallas_call x1, Pallas kernels, local(): pl.pallas_call(assemble, out_shape=(jax.ShapeDtypeStruct((BLK, BLK), BF16...  2.21 us

profile of v5, /device:TPU:2, one launch (start us, length us, event | category | flops | bytes accessed | tf_op | source)
XLA Modules:
  0.0 48.8 jit_solution(411165943455979459)
XLA Ops:
  0.6 46.0 %hyena.1 = (bf16[32,16,128]{2,1,0:T(8,128)(2,1)S(1)}, f32[32,1,128]{2,1,0:T(1,128)S(1)}, bf16[4,8,16,128]{3,2,1,0:T(8,128)(2,1)S(1)}) custom-call(bf16[128,128]{1,0:T(8,128)(2,1)} %q_hbm.1, bf16[128,128]{1,0:T(8,128)(2,1)} %k_hbm.1, bf16[128,128]{1,0:T(8,128)(2,1)} %c_hbm.1, bf16[128,128]{1,0:T(8,128)(2,1)} %v_hbm.1, f32[3,7,128]{2,1,0:T(8,128)} %taps_hbm.1, ...), custom_call_target="tpu_custom_call" | custom-call | tf_op jit(solution)/shard_map/hyena/pallas_call | solution.py:482
  46.6 2.2 %assemble.1 = (bf16[128,128]{1,0:T(8,128)(2,1)}, bf16[3,128,128]{2,1,0:T(8,128)(2,1)}, f32[3,7,128]{2,1,0:T(8,128)}, f32[1,128]{1,0:T(1,128)}, f32[8,6144]{1,0:T(8,128)}) custom-call(bf16[32,16,128]{2,1,0:T(8,128)(2,1)S(1)} %get-tuple-element.13.back_hbm, f32[32,1,128]{2,1,0:T(1,128)S(1)} %get-tuple-element.14.small_hbm, ...), custom_call_target="tpu_custom_call" | custom-call | tf_op jit(solution)/shard_map/assemble/pallas_call | solution.py:530

commit v6 on v5

--- a/solution.py
+++ b/solution.py
@@ -132,7 +132,7 @@
     def _():
         pl.semaphore_wait(barrier, NW)
 
-    for zp in range(NW // 4):
+    for zp in reversed(range(NW // 4)):
         @pl.when(zp <= plane)
         def _(zp=zp):
             send_in(zp)
@@ -422,26 +422,17 @@
 
 
 def assemble(
-    back_hbm, small_hbm, fg_hbm,
+    backb, smallb, fgbuf,
     out_ref, ig_ref, tapg_ref, skipg_ref, fg_ref,
-    backb, smallb, fgbuf, fg_s, sm_s, sems,
+    fg_s, sm_s,
 ):
-    loads = [
-        pltpu.make_async_copy(back_hbm, backb, sems.at[0]),
-        pltpu.make_async_copy(small_hbm, smallb, sems.at[1]),
-        pltpu.make_async_copy(fg_hbm, fgbuf, sems.at[2]),
-    ]
-    for load in loads:
-        load.start()
     perm = transposer()
-    loads[0].wait()
     back = dot(backb[...].reshape(512, BLK), perm, ((0,), (0,))).astype(BF16)
     ig_ref[0] = back[:, 0:128]
     ig_ref[1] = back[:, 128:256]
     out_ref[...] = back[:, 256:384]
     ig_ref[2] = back[:, 384:512]
 
-    loads[1].wait()
     sm_s[...] = jnp.zeros((BLK, BLK), F32)
     for m in range(NW):
         sm_s[m : m + 1, :] = smallb[m]
@@ -458,7 +449,6 @@
         if stream == 0:
             skipg_ref[...] = picked[TAPS:]
 
-    loads[2].wait()
     fg_s[...] = fgbuf[...].astype(F32)
     for part in range(4):
         def lay(n, carry, part=part):
@@ -536,15 +526,11 @@
             jax.ShapeDtypeStruct((1, BLK), F32),
             jax.ShapeDtypeStruct((NG, NB * BLK), F32),
         ),
-        in_specs=[anywhere] * 3,
+        in_specs=[vmem] * 3,
         out_specs=(vmem,) * 5,
         scratch_shapes=[
-            pltpu.VMEM((NW, 16, BLK), BF16),
-            pltpu.VMEM((NW, 1, BLK), F32),
-            pltpu.VMEM((4, NG, 16, BLK), BF16),
             pltpu.VMEM((4, NG, 16, BLK), F32),
             pltpu.VMEM((BLK, BLK), F32),
-            dma((3,)),
         ],
         compiler_params=pltpu.CompilerParams(vmem_limit_bytes=8 << 20),
         name="assemble",

time: 49 us -> 48 us (0.980)
  Pallas kernels: 48.2 us -> 47.2 us
    pallas_call x1, Pallas kernels: 2.21 us -> 1.43 us  [local(): pl.pallas_call(assemble, out_shape=(jax.ShapeDtypeStruct((BLK, BLK), BF16...]
where the time goes in v6:
time: 48 us; the launch traced here: 47.8 us
  Pallas kernels  47.2 us (98%)
  between operations  0.64 us (1%)
    pallas_call x1, Pallas kernels, local(): pl.pallas_call(kernel, out_shape=raw, in_specs=[pl.BlockSpec(memory_space...  45.8 us
    pallas_call x1, Pallas kernels, local(): pl.pallas_call(assemble, out_shape=(jax.ShapeDtypeStruct((BLK, BLK), BF16...  1.43 us

profile of v6, /device:TPU:2, one launch (start us, length us, event | category | flops | bytes accessed | tf_op | source)
XLA Modules:
  0.0 47.8 jit_solution(428968331543951167)
XLA Ops:
  0.6 45.8 %hyena.1 = (bf16[32,16,128]{2,1,0:T(8,128)(2,1)S(1)}, f32[32,1,128]{2,1,0:T(1,128)S(1)}, bf16[4,8,16,128]{3,2,1,0:T(8,128)(2,1)S(1)}) custom-call(bf16[128,128]{1,0:T(8,128)(2,1)} %q_hbm.1, bf16[128,128]{1,0:T(8,128)(2,1)} %k_hbm.1, bf16[128,128]{1,0:T(8,128)(2,1)} %c_hbm.1, bf16[128,128]{1,0:T(8,128)(2,1)} %v_hbm.1, f32[3,7,128]{2,1,0:T(8,128)} %taps_hbm.1, ...), custom_call_target="tpu_custom_call" | custom-call | tf_op jit(solution)/shard_map/hyena/pallas_call | solution.py:472
  46.4 1.4 %assemble.1 = (bf16[128,128]{1,0:T(8,128)(2,1)}, bf16[3,128,128]{2,1,0:T(8,128)(2,1)}, f32[3,7,128]{2,1,0:T(8,128)}, f32[1,128]{1,0:T(1,128)}, f32[8,6144]{1,0:T(8,128)}) custom-call(bf16[32,16,128]{2,1,0:T(8,128)(2,1)S(1)} %get-tuple-element.13.backb, f32[32,1,128]{2,1,0:T(1,128)S(1)} %get-tuple-element.14.smallb, ...), custom_call_target="tpu_custom_call" | custom-call | tf_op jit(solution)/shard_map/assemble/pallas_call | solution.py:520
